TPU v7x, 256 devices: a whole 4x4x8 slice. The times are simulated.
256 devices in a mesh: bins: 16 (over y, z_hi, core), batch: 16 (over x, z_lo).
Axes of the slice: x: 4, y: 4, z: 8 (z_hi: 2, z_lo: 4; z = z_hi * 4 + z_lo), core: 2. Of those that a mesh axis runs over, the one named last changes fastest.
Arguments:
- features: bfloat16 [16, 4096, 1536], P('batch', 'bins'), may hold values from -6 to 6
- norm_gain: float32 [1536], replicated, may hold values from 0.25 to 1.75
- convolution_taps_weight: bfloat16 [3, 1536, 768], replicated, may hold values from -0.09375 to 0.09375
- out_weight: bfloat16 [768, 1536], replicated, may hold values from -0.21875 to 0.21875
- head_weight: bfloat16 [1536, 4096], P(None, 'batch'), may hold values from -0.15625 to 0.15625
- rc_perm: int32 [1536], replicated, may hold values from 0 to 1535, each once
- exon_bins: int32 [16, 64, 8], P('batch'), may hold values from 0 to 4095, as said below
- exon_count: int32 [16, 64], P('batch'), may hold values from 1 to 8
- gene_strand: int32 [16, 64], P('batch'), may hold values 0 or 1
- gene_target: float32 [16, 64, 4096], P('batch', 'bins'), may hold values from 0.5 to 8
Outputs:
- input_grad: bfloat16 [16, 4096, 1536], P('batch', 'bins')
- out_weight_grad: float32 [768, 1536], P('batch')
Inputs may be any that keep to these rules, and one draw needn't show every extreme that they name: `rc_perm`: a permutation of the channels. `exon_bins`: bins of the gene's own sequence; a bin may be listed more than once; each gene's listed bins lie within 256 consecutive bins. All genes of a sequence may lie within the same 256 bins j * 256 to (j + 1) * 256 - 1 of one j, and then every one of those bins may be listed and counted.
All inputs are finite; a program needn't handle non-finite values. No bound on the sum of `gene_strand` on one device may be relied on, other than what follows from the above.
Results may differ from a plain program's by a relative error of at most 0.014.
Values may be sent and summed in bfloat16 or wider, within the bound.
No kernel may reach another device: no remote copies, remote signals or barrier semaphores. Data moves between devices by JAX's collectives and lax.ppermute only.
A program may use at most 128 MiB of HBM per device.

v0:
```python
import jax
import jax.numpy as jnp
from jax import lax
from jax.experimental import pallas as pl
from jax.experimental.pallas import tpu as pltpu
from jax.sharding import Mesh
from jax.sharding import PartitionSpec as P

DILATION_STEP = 16
BINS = ("y", "zh", "core")


def shifted(block, axis, shift):
    count = lax.axis_size(axis)
    return lax.ppermute(block, axis, [(i, (i + shift) % count) for i in range(count)])


def edge_rows(block, width):
    count = lax.axis_size(BINS)
    low = lax.ppermute(block[-width:], BINS, [(i, i + 1) for i in range(count - 1)])
    high = lax.ppermute(block[:width], BINS, [(i + 1, i) for i in range(count - 1)])
    return low, high


def pick(stack, index):
    return lax.dynamic_index_in_dim(stack, index, 0, keepdims=False)


def wide(value):
    return value.astype(jnp.float32)


def narrow(value):
    return value.astype(jnp.bfloat16)


def gelu_slope(argument):
    return (
        0.5 * (1.0 + jax.scipy.special.erf(argument * 0.7071067811865476))
        + argument * jnp.exp(-0.5 * argument * argument) * 0.3989422804014327
    )


def dot(left, right, over=(1, 0)):
    return lax.dot_general(
        left, right, (((over[0],), (over[1],)), ((), ())), preferred_element_type=jnp.float32
    )


INTERPRET = False
NORM_ROWS = 16


def gelu(argument):
    return 0.5 * argument * (1.0 + lax.erf(argument * 0.7071067811865476))


def block_columns(
    edge_ref, rows_ref, gain_ref, taps_hbm, out_hbm, taps_ref, out_ref, hidden_ref, active_ref,
    sems, put, emit, before_emit=None,
):
    taps_copy = pltpu.make_async_copy(taps_hbm, taps_ref, sems.at[0])
    out_copy = pltpu.make_async_copy(out_hbm, out_ref, sems.at[1])
    taps_copy.start()
    out_copy.start()
    count, channels = rows_ref.shape
    width = out_ref.shape[0]

    def normalize_some(value):
        value = wide(value)
        inverse = lax.rsqrt(jnp.mean(value * value, axis=-1, keepdims=True) + 1e-06)
        return narrow(gelu(value * inverse * gain_ref[...]))

    def normalize_rows(i, carry):
        start = pl.multiple_of(i * NORM_ROWS, NORM_ROWS)
        hidden_ref[pl.ds(start + DILATION_STEP, NORM_ROWS), :] = normalize_some(
            rows_ref[pl.ds(start, NORM_ROWS), :]
        )
        return carry

    hidden_ref[:DILATION_STEP, :] = normalize_some(edge_ref[:DILATION_STEP, :])
    hidden_ref[DILATION_STEP + count :, :] = normalize_some(edge_ref[DILATION_STEP:, :])
    lax.fori_loop(0, count // NORM_ROWS, normalize_rows, 0, unroll=2)
    taps_copy.wait()
    block = min(256, width)

    def columns(j):
        return pl.ds(pl.multiple_of(j * block, block), block)

    def convolve(j, carry):
        cut = columns(j)
        total = jnp.zeros((count, block), jnp.float32)
        for tap in range(3):
            total += dot(
                hidden_ref[tap * DILATION_STEP : tap * DILATION_STEP + count, :],
                taps_ref[tap, :, cut],
            )
        put(cut, total)
        return carry

    lax.fori_loop(0, width // block, convolve, 0)
    out_copy.wait()

    def project(j, carry):
        cut = columns(j)
        emit(cut, narrow(wide(rows_ref[:, cut]) + dot(active_ref[...], out_ref[:, cut])))
        return carry

    if before_emit:
        before_emit()
    lax.fori_loop(0, channels // block, project, 0)


def forward_kernel(
    base_ref, edge_ref, rows_ref, gain_ref, entry_ref, taps_hbm, out_hbm,
    kept_ref, sent_ref, active_ref, block_hbm, sum_hbm,
    taps_ref, out_ref, hidden_ref, pick_ref, block_ref, sum_ref, sems,
):
    count, channels = block_ref.shape
    sum_copy = pltpu.make_async_copy(sum_ref, sum_hbm, sems.at[2])
    block_copy = pltpu.make_async_copy(block_ref, block_hbm, sems.at[3])
    entries = entry_ref.shape[1]
    half = entries // 2
    row = base_ref[0] + lax.broadcasted_iota(jnp.int32, (count, entries), 0)
    pick_ref[...] = narrow(jnp.where(entry_ref[...] == row, 1.0, 0.0))
    core = base_ref[1]
    own = pick_ref.at[:, pl.ds(pl.multiple_of(core * half, half), half)]
    other = pick_ref.at[:, pl.ds(pl.multiple_of((1 - core) * half, half), half)]

    def put(cut, total):
        sum_ref[:, cut] = total
        active_ref[:, cut] = narrow(gelu(total))

    def emit(cut, part):
        block_ref[:, cut] = part
        sent_ref[:, cut] = narrow(dot(other[...], part, (0, 0)))
        kept_ref[:, cut] = narrow(dot(own[...], part, (0, 0)))

    block_columns(
        edge_ref, rows_ref, gain_ref, taps_hbm, out_hbm, taps_ref, out_ref, hidden_ref, active_ref,
        sems, put, emit, sum_copy.start,
    )
    block_copy.start()
    sent_ref[:, channels:] = narrow(dot(other[...], active_ref[...], (0, 0)))
    kept_ref[:, channels:] = narrow(dot(own[...], active_ref[...], (0, 0)))
    sum_copy.wait()
    block_copy.wait()


def reflect_kernel(
    padded_ref, gain_ref, own_ref, perm_ref, taps_hbm, out_hbm, wide_ref, narrow_ref,
    taps_ref, out_ref, hidden_ref, active_ref, partner_ref, mirror_ref, sems,
):
    count, channels = own_ref.shape
    edge_ref = padded_ref.at[: 2 * DILATION_STEP, :]
    rows_ref = padded_ref.at[2 * DILATION_STEP :, :]

    def put(cut, total):
        active_ref[:, cut] = narrow(gelu(total))

    def emit(cut, part):
        partner_ref[:, cut] = part

    block_columns(
        edge_ref, rows_ref, gain_ref, taps_hbm, out_hbm, taps_ref, out_ref, hidden_ref, active_ref,
        sems, put, emit,
    )
    place = lax.broadcasted_iota(jnp.int32, (count, count), 0)
    other = lax.broadcasted_iota(jnp.int32, (count, count), 1)
    reversal = narrow(jnp.where(place + other == count - 1, 1.0, 0.0))
    mirror_ref[...] = narrow(dot(reversal, partner_ref[...]))
    wide_ref[...] = wide(own_ref[...])
    some = min(256, channels)

    def mix(j, carry):
        cut = pl.ds(pl.multiple_of(j * some, some), some)
        channel = j * some + lax.broadcasted_iota(jnp.int32, (some, channels), 0)
        chosen = narrow(jnp.where(perm_ref[...] == channel, 1.0, 0.0))
        wide_ref[...] -= 0.5 * dot(mirror_ref[:, cut], chosen)
        wide_ref[:, cut] -= 0.5 * dot(mirror_ref[...], chosen, (1, 1))
        return carry

    lax.fori_loop(0, channels // some, mix, 0)
    narrow_ref[...] = narrow(wide_ref[...])


def reflect(padded, norm_gain, block_out, rc_perm, taps, out_weight):
    count, channels = block_out.shape
    vmem = pl.BlockSpec(memory_space=pltpu.VMEM)
    bf = jnp.bfloat16
    return pl.pallas_call(
        reflect_kernel,
        out_shape=[
            jax.ShapeDtypeStruct((count, channels), jnp.float32),
            jax.ShapeDtypeStruct((count, channels), bf),
        ],
        in_specs=[vmem] * 4 + [pl.BlockSpec(memory_space=pltpu.HBM)] * 2,
        out_specs=[vmem] * 2,
        scratch_shapes=[
            pltpu.VMEM(taps.shape, bf),
            pltpu.VMEM(out_weight.shape, bf),
            pltpu.VMEM((count + 2 * DILATION_STEP, channels), bf),
            pltpu.VMEM((count, out_weight.shape[0]), bf),
            pltpu.VMEM((count, channels), bf),
            pltpu.VMEM((count, channels), bf),
            pltpu.SemaphoreType.DMA((2,)),
        ],
        compiler_params=pltpu.CompilerParams(vmem_limit_bytes=20 << 20),
        cost_estimate=pl.CostEstimate(
            flops=count * channels * (8 * out_weight.shape[0] + 4 * channels),
            transcendentals=count * channels,
            bytes_accessed=2 * (taps.size + out_weight.size) + 10 * count * channels,
        ),
        name="reflect",
        interpret=INTERPRET,
    )(
        padded,
        norm_gain[None, :],
        block_out,
        rc_perm[None, :],
        in_hbm(taps),
        in_hbm(out_weight),
    )


def hbm(shape, kind):
    return jax.ShapeDtypeStruct(shape, kind) if INTERPRET else pltpu.HBM(shape, kind)


def in_hbm(value):
    return value if INTERPRET else pltpu.with_memory_space_constraint(value, pltpu.HBM)


def forward(edges, rows, norm_gain, entry_bins, base, taps, out_weight):
    count, channels = rows.shape
    width = out_weight.shape[0]
    entries = entry_bins.shape[0]
    vmem = pl.BlockSpec(memory_space=pltpu.VMEM)
    bf = jnp.bfloat16
    payload = jax.ShapeDtypeStruct((entries // 2, channels + width), bf)
    return pl.pallas_call(
        forward_kernel,
        out_shape=[
            payload,
            payload,
            jax.ShapeDtypeStruct((count, width), bf),
            hbm((count, channels), bf),
            hbm((count, width), jnp.float32),
        ],
        in_specs=[pl.BlockSpec(memory_space=pltpu.SMEM), vmem, vmem, vmem, vmem]
        + [pl.BlockSpec(memory_space=pltpu.HBM)] * 2,
        out_specs=[vmem] * 3 + [pl.BlockSpec(memory_space=pltpu.HBM)] * 2,
        scratch_shapes=[
            pltpu.VMEM(taps.shape, bf),
            pltpu.VMEM(out_weight.shape, bf),
            pltpu.VMEM((count + 2 * DILATION_STEP, channels), bf),
            pltpu.VMEM((count, entries), bf),
            pltpu.VMEM((count, channels), bf),
            pltpu.VMEM((count, width), jnp.float32),
            pltpu.SemaphoreType.DMA((4,)),
        ],
        compiler_params=pltpu.CompilerParams(vmem_limit_bytes=20 << 20),
        cost_estimate=pl.CostEstimate(
            flops=2 * count * (4 * channels * width + entries * (channels + width)),
            transcendentals=count * (channels + width),
            bytes_accessed=2 * (taps.size + out_weight.size) + 8 * count * channels,
        ),
        name="forward",
        interpret=INTERPRET,
    )(
        base,
        edges,
        rows,
        norm_gain[None, :],
        entry_bins[None, :],
        in_hbm(taps),
        in_hbm(out_weight),
    )


def after(value, token):
    return lax.optimization_barrier((value, token))[0]


def gather_head(head_weight):
    core = lax.axis_index("core")
    half = head_weight.shape[1] // 2
    mine = jnp.where(core == 0, head_weight[:, :half], head_weight[:, half:]).T
    pieces = [shifted(mine, "x", k) for k in range(1, lax.axis_size("x"))]
    held = jnp.concatenate([mine] + pieces, axis=0)
    return held, shifted(held, "core", 1)


def deal_targets(gene_target, own_strand, own_count):
    nx, nz = lax.axis_size("x"), lax.axis_size("zl")
    x, zl, core = (lax.axis_index(a) for a in ("x", "zl", "core"))
    genes, tracks = gene_target.shape
    odd = (lax.broadcasted_iota(jnp.int32, gene_target.shape, 1) & 1) == 1
    swapped = jnp.where(odd, jnp.roll(gene_target, 1, axis=1), jnp.roll(gene_target, -1, axis=1))
    flipped = jnp.where(own_strand[:, None] == 1, swapped, gene_target)
    parts = flipped.reshape(genes, nx, nz, 2, tracks // (nx * nz * 2))
    parts = jnp.transpose(parts, (1, 2, 0, 3, 4))
    parts = jnp.where(core == 0, parts, parts[:, :, :, ::-1])
    parts = jnp.stack([pick(parts, (x - k) % nx) for k in range(nx)], axis=3)
    parts = parts.reshape(nz, genes, tracks // nz)
    counts = jnp.broadcast_to(wide(own_count)[None, :, None], (nz, genes, 128))
    parts = jnp.concatenate([parts, counts], axis=2)
    parts = lax.all_to_all(parts, "zl", split_axis=0, concat_axis=0, tiled=True)
    return jnp.concatenate([pick(parts, (zl - k) % nz) for k in range(nz)], axis=0)


def listed_bins(exon_bins, exon_count):
    place = lax.broadcasted_iota(jnp.int32, exon_bins.shape, 1)
    return jnp.where(place < exon_count[:, None], exon_bins, -1)


def by_owner(entry_bins):
    ny, nh, nc = (lax.axis_size(a) for a in BINS)
    return entry_bins.reshape(ny, nh, nc, -1).transpose(2, 0, 1, 3).reshape(-1)


def by_distance(entry_bins):
    ny, nh, nc = (lax.axis_size(a) for a in BINS)
    y, zh, core = (lax.axis_index(a) for a in BINS)
    devices = ny * nh * nc
    owner = lax.iota(jnp.int32, devices)
    owner_core = (core + owner // (ny * nh)) % nc
    owner_y = (y + (owner // nh) % ny) % ny
    owner_zh = (zh + owner % nh) % nh
    owner = (owner_y * nh + owner_zh) * nc + owner_core
    entry_bins = entry_bins.reshape(devices, -1)
    chosen = owner[:, None] == lax.iota(jnp.int32, devices)[None, :]
    return jnp.sum(jnp.where(chosen[:, :, None], entry_bins[None], 0), axis=1).reshape(-1)


def whole_step(
    features,
    norm_gain,
    convolution_taps_weight,
    out_weight,
    head_weight,
    rc_perm,
    exon_bins,
    exon_count,
    gene_strand,
    gene_target,
):
    ny, nh, nc, nx, nz = (lax.axis_size(a) for a in ("y", "zh", "core", "x", "zl"))
    y, zh, core, x, _ = (lax.axis_index(a) for a in ("y", "zh", "core", "x", "zl"))
    bin_devices = ny * nh * nc
    bin_index = (y * nh + zh) * nc + core
    rows = features[0]
    count_of_rows, channels = rows.shape
    low, high = edge_rows(rows, DILATION_STEP)
    head, head_other = gather_head(head_weight)
    entry_bins = listed_bins(exon_bins[0], exon_count[0])
    entries = entry_bins.size
    edges = jnp.concatenate([low, high], axis=0)
    partner = lax.ppermute(
        jnp.concatenate([edges, rows], axis=0),
        BINS,
        [(i, bin_devices - 1 - i) for i in range(bin_devices)],
    )
    kept, sent, active, block_out, convolved_sum = forward(
        edges,
        rows,
        norm_gain,
        by_owner(entry_bins),
        jnp.stack([bin_index * count_of_rows, core]),
        convolution_taps_weight,
        out_weight,
    )

    sent = shifted(sent, "core", 1)
    sent = narrow(wide(kept) + wide(sent)).reshape(ny, -1, kept.shape[1])
    pieces = [shifted(pick(sent, (y + k) % ny), "y", k) for k in range(1, ny)]
    sent = narrow(wide(pick(sent, y)) + sum(wide(piece) for piece in pieces))
    sent = sent.reshape(nh, -1, kept.shape[1])
    piece = shifted(pick(sent, 1 - zh), "zh", 1)
    sent = narrow(wide(pick(sent, zh)) + wide(piece))
    gathered = jnp.concatenate([sent] + [shifted(sent, "zl", k) for k in range(1, nz)], axis=0)
    gathered_active = gathered[:, channels:]
    gathered = gathered[:, :channels]

    distant_bins = by_distance(after(entry_bins, block_out))
    positions = bin_index * count_of_rows + lax.iota(jnp.int32, count_of_rows)
    pick_rows = narrow(distant_bins[None, :] == positions[:, None])
    own_genes = exon_bins.shape[1] // bin_devices
    gene_strand, exon_count = after((gene_strand, exon_count), block_out)
    own_strand = lax.dynamic_slice_in_dim(gene_strand[0], bin_index * own_genes, own_genes, 0)
    own_count = lax.dynamic_slice_in_dim(exon_count[0], bin_index * own_genes, own_genes, 0)
    targets = deal_targets(after(gene_target[0], block_out), own_strand, own_count)
    rc_grad, rc_narrow = reflect(
        partner,
        norm_gain,
        block_out,
        rc_perm,
        convolution_taps_weight,
        out_weight,
    )

    logits = jnp.concatenate([dot(gathered, head, (1, 1)), dot(gathered, head_other, (1, 1))], axis=1)
    grouped = (nz * own_genes, exon_bins.shape[2], logits.shape[1])
    tracks = logits.shape[1]
    predicted = narrow(jax.nn.softplus(logits)).reshape(grouped)
    counted = lax.broadcasted_iota(jnp.int32, grouped[:2], 1) < targets[:, tracks:tracks + 1].astype(
        jnp.int32
    )
    coverage = jnp.sum(jnp.where(counted[:, :, None], wide(predicted), 0.0), axis=1)
    spread_back = narrow(1.0 - targets[:, :tracks] / (1.0 + coverage))
    logit_grad = narrow(
        wide(spread_back)[:, None, :] * jax.nn.sigmoid(logits).reshape(grouped)
    ).reshape(logits.shape)
    entry_grad = narrow(
        dot(logit_grad[:, : tracks // 2], head) + dot(logit_grad[:, tracks // 2 :], head_other)
    )
    back = entry_grad.reshape(nz, -1, channels)
    pieces = [shifted(back[k], "zl", -k) for k in range(1, nz)]
    back = narrow(wide(back[0]) + sum(wide(piece) for piece in pieces))
    back = jnp.concatenate([back, shifted(back, "zh", 1)], axis=0)
    back = jnp.concatenate([back] + [shifted(back, "y", -k) for k in range(1, ny)], axis=0)
    back_other = shifted(back, "core", 1)
    head_back = dot(pick_rows[:, : entries // 2], back) + dot(
        pick_rows[:, entries // 2 :], back_other
    )
    block_grad = narrow(head_back + rc_grad)

    half = channels // 2

    def turn(value):
        return jnp.where(core == 0, value, jnp.roll(value, half, axis=1))

    turned, turned_entries = turn(rc_narrow), turn(entry_grad)

    def share_of(cut):
        return dot(active, turned[:, cut], (0, 0)) + dot(
            gathered_active, turned_entries[:, cut], (0, 0)
        )

    piece = shifted(narrow(share_of(slice(half, None))), "core", 1)
    share = narrow(share_of(slice(0, half)) + wide(piece)).reshape(nx, -1, half)
    pieces = [shifted(pick(share, (x + k) % nx), "x", k) for k in range(1, nx)]
    share = wide(pick(share, x)) + sum(wide(piece) for piece in pieces)
    share = narrow(share).reshape(nz, -1, half)
    pieces = lax.all_to_all(share, "zl", split_axis=0, concat_axis=0, tiled=True)
    share = narrow(jnp.sum(wide(pieces), axis=0))
    share = narrow(
        (wide(share) + wide(shifted(share, "y", 2)))
        + (wide(shifted(share, "y", 1)) + wide(shifted(share, "y", 3)))
    )
    share = wide(share) + wide(shifted(share, "zh", 1))
    other = shifted(share, "core", 1)
    out_weight_grad = jnp.concatenate(
        [jnp.where(core == 0, share, other), jnp.where(core == 0, other, share)], axis=1
    )

    activation_gradient = narrow(dot(block_grad, out_weight, (1, 1)) * gelu_slope(convolved_sum))
    low, high = edge_rows(activation_gradient, DILATION_STEP)
    padded_gradient = jnp.concatenate([low, activation_gradient, high], axis=0)
    hidden_grad = jnp.zeros((count_of_rows, channels), jnp.float32)
    for tap in range(3):
        start = (2 - tap) * DILATION_STEP
        hidden_grad = hidden_grad + dot(
            padded_gradient[start : start + count_of_rows], convolution_taps_weight[tap], (1, 1)
        )
    widened = wide(after(rows, block_out))
    inverse = lax.rsqrt(jnp.mean(widened * widened, axis=-1, keepdims=True) + 1e-06)
    normed = widened * inverse * norm_gain
    normed_grad = hidden_grad * gelu_slope(normed) * norm_gain
    norm_back = inverse * normed_grad - widened * inverse**3 * jnp.mean(
        normed_grad * widened, axis=-1, keepdims=True
    )
    input_grad = narrow(wide(block_grad) + norm_back)
    return (input_grad[None], out_weight_grad)


def solution(mesh):
    cut = Mesh(mesh.devices.reshape(4, 2, 2, 4, 4), BINS + ("x", "zl"))
    batch = ("x", "zl")
    in_specs = (
        P(batch, BINS, None),
        P(),
        P(),
        P(),
        P(None, batch),
        P(),
        P(batch, None, None),
        P(batch, None),
        P(batch, None),
        P(batch, BINS, None),
    )
    out_specs = (P(batch, BINS, None), P(batch, None))
    return jax.shard_map(
        whole_step, mesh=cut, in_specs=in_specs, out_specs=out_specs, check_vma=False
    )
```

profile of v0, /device:TPU:1, one launch (start us, length us, event | category | flops | bytes accessed | tf_op | source)
XLA Modules:
  0.0 227.1 jit_solution(14265668808917908222)
XLA Ops:
  0.7 2.0 select_bitcast_fusion
  2.6 3.3 %collective-permute-start.12 = (bf16[128,1536]{0,1:T(8,128)(2,1)}, bf16[128,1536]{0,1:T(8,128)(2,1)}, u32[]{:S(2)}, u32[]{:S(2)}) collective-permute-start(bf16[128,1536]{0,1:T(8,128)(2,1)} %select_bitcast_fusion), channel_id=1, source_target_pairs={{0,12},{4,0},{8,4},{12,8},{1,13},{5,1},{9,5},{13,9},{2,14},{6,2},{... | collective-permute-start | bytes 1179656 | tf_op jit(solution)/shard_map/ppermute | solution.py:15
  7.9 10.2 %collective-permute-start = (bf16[16,1536]{1,0:T(8,128)(2,1)S(1)}, bf16[16,1536]{1,0:T(8,128)(2,1)S(1)}, u32[]{:S(2)}, u32[]{:S(2)}) collective-permute-start(bf16[16,1536]{1,0:T(8,128)(2,1)S(1)} %get-tuple-element.36), channel_id=1, source_target_pairs={{0,16},{16,32},{32,48},{48,64},{64,80},{80,96},{96,112},{112,128},... | collective-permute-start | bytes 147464 | tf_op jit(solution)/shard_map/ppermute | solution.py:20
  18.1 1.9 collective-permute-start.1
  27.5 10.5 %forward.1 = (bf16[256,2304]{1,0:T(8,128)(2,1)S(1)}, bf16[256,2304]{1,0:T(8,128)(2,1)S(1)}, bf16[256,768]{1,0:T(8,128)(2,1)S(1)}, bf16[256,1536]{1,0:T(8,128)(2,1)}, f32[256,768]{1,0:T(8,128)}) custom-call(s32[2]{0:T(128)S(1)} %pad_add_fusion.base_ref, bf16[32,1536]{1,0:T(8,128)(2,1)S(1)} %pad_maximum_fusion.11.edge_ref, bf16[256,1536]{1,0:T(8,128)(2,1)S(1)} %bitcast.97, ...), custom_call_target="tpu_custom_call" | custom-call | flops 3019898880 | bytes 12582912 | tf_op jit(solution)/shard_map/forward/pallas_call | solution.py:241
  41.4 7.4 %collective-permute-start.22 = (bf16[288,1536]{1,0:T(8,128)(2,1)}, bf16[288,1536]{1,0:T(8,128)(2,1)}, u32[]{:S(2)}, u32[]{:S(2)}) collective-permute-start(bf16[288,1536]{1,0:T(8,128)(2,1)} %pad_maximum_fusion.1), channel_id=1, source_target_pairs={{0,240},{16,224},{32,208},{48,192},{64,176},{80,160},{96,144},{112... | collective-permute-start | bytes 2654216 | tf_op jit(solution)/shard_map/ppermute | solution.py:359
  56.4 1.6 fusion.64
  58.0 1.5 reshape.225
  59.6 1.5 copy.43
  61.0 1.6 rev.3
  64.3 1.5 reshape.226
  66.4 1.5 pad_maximum_fusion.12
  67.9 3.9 %all-to-all-start = ((f32[4,4,1152]{2,1,0:T(4,128)}), f32[4,4,1152]{2,1,0:T(4,128)}, u32[]{:S(2)}, u32[]{:S(2)}) async-start(f32[4,4,1152]{2,1,0:T(4,128)} %pad_maximum_fusion.12), calls=%async_computation | async-start | bytes 147456 | tf_op jit(solution)/shard_map/all_to_all | solution.py:308
  71.9 1.5 broadcast_compare_fusion
  74.7 13.0 %all-to-all-done = f32[4,4,1152]{2,1,0:T(4,128)} async-done(((f32[4,4,1152]{2,1,0:T(4,128)}), f32[4,4,1152]{2,1,0:T(4,128)}, u32[]{:S(2)}, u32[]{:S(2)}) %all-to-all-start) | async-done | bytes 73760 | tf_op jit(solution)/shard_map/all_to_all | solution.py:308
  88.8 1.5 pad_maximum_fusion
  90.4 1.5 add_convert_fusion.2
  92.0 2.4 %collective-permute-start.3 = (bf16[64,2304]{1,0:T(8,128)(2,1)S(1)}, bf16[64,2304]{1,0:T(8,128)(2,1)S(1)}, u32[]{:S(2)}, u32[]{:S(2)}) collective-permute-start(bf16[64,2304]{1,0:T(8,128)(2,1)S(1)} %get-tuple-element.31), channel_id=1, source_target_pairs={{0,64},{64,128},{128,192},{192,0},{1,65},{65,129},{129,193},{193,1... | collective-permute-start | bytes 884744 | tf_op jit(solution)/shard_map/ppermute | solution.py:15
  94.8 1.9 collective-permute-start.4
  96.7 12.3 %reflect.1 = (f32[256,1536]{1,0:T(8,128)S(1)}, bf16[256,1536]{1,0:T(8,128)(2,1)S(1)}) custom-call(bf16[288,1536]{1,0:T(8,128)(2,1)} %collective-permute-done.22.padded_ref, f32[1,1536]{1,0:T(1,128)S(1)} %broadcast_in_dim.75.gain_ref, bf16[256,1536]{1,0:T(8,128)(2,1)S(1)} %copy-done.3, s32[1,1536]{1,0:T(1,128)S(1)} %broadcast_in_dim.83.perm_ref, ...), custom_call_target="tpu_custom_call" | custom-call | flops 4831838208 | bytes 13369344 | tf_op jit(solution)/shard_map/reflect/pallas_call | solution.py:191
  109.2 3.6 %collective-permute-start.6 = (bf16[32,2304]{1,0:T(8,128)(2,1)S(1)}, bf16[32,2304]{1,0:T(8,128)(2,1)S(1)}, u32[]{:S(2)}, u32[]{:S(2)}) collective-permute-start(bf16[32,2304]{1,0:T(8,128)(2,1)S(1)} %dynamic-slice_bitcast_fusion.6), channel_id=1, source_target_pairs={{0,32},{32,0},{1,33},{33,1},{2,34},{34,2},{3,35},{35,3},{4,36},{36... | collective-permute-start | bytes 442376 | tf_op jit(solution)/shard_map/ppermute | solution.py:15
  112.8 7.4 %collective-permute-done.6 = bf16[32,2304]{1,0:T(8,128)(2,1)S(1)} collective-permute-done((bf16[32,2304]{1,0:T(8,128)(2,1)S(1)}, bf16[32,2304]{1,0:T(8,128)(2,1)S(1)}, u32[]{:S(2)}, u32[]{:S(2)}) %collective-permute-start.6) | collective-permute-done | bytes 147488 | tf_op jit(solution)/shard_map/ppermute | solution.py:15
  120.3 4.2 %collective-permute-start.9 = (bf16[32,2304]{1,0:T(8,128)(2,1)S(1)}, bf16[32,2304]{1,0:T(8,128)(2,1)S(1)}, u32[]{:S(2)}, u32[]{:S(2)}) collective-permute-start(bf16[32,2304]{1,0:T(8,128)(2,1)S(1)} %fusion.51), channel_id=1, source_target_pairs={{0,3},{1,0},{2,1},{3,2},{4,7},{5,4},{6,5},{7,6},{8,11},{9,8},{10,9... | collective-permute-start | bytes 442376 | tf_op jit(solution)/shard_map/ppermute | solution.py:15
  125.1 1.5 collective-permute-done.9
  126.6 9.9 %collective-permute-done.8 = bf16[32,2304]{1,0:T(8,128)(2,1)S(1)} collective-permute-done((bf16[32,2304]{1,0:T(8,128)(2,1)S(1)}, bf16[32,2304]{1,0:T(8,128)(2,1)S(1)}, u32[]{:S(2)}, u32[]{:S(2)}) %collective-permute-start.8) | collective-permute-done | bytes 147488 | tf_op jit(solution)/shard_map/ppermute | solution.py:15
  140.9 2.6 %collective-permute-start.15 = (bf16[32,1536]{1,0:T(8,128)(2,1)S(1)}, bf16[32,1536]{1,0:T(8,128)(2,1)S(1)}, u32[]{:S(2)}, u32[]{:S(2)}) collective-permute-start(bf16[32,1536]{1,0:T(8,128)(2,1)S(1)} %get-tuple-element.44), channel_id=1, source_target_pairs={{0,2},{1,3},{2,0},{3,1},{4,6},{5,7},{6,4},{7,5},{8,10},{9,11},{10,... | collective-permute-start | bytes 294920 | tf_op jit(solution)/shard_map/ppermute | solution.py:15
  144.0 2.5 %collective-permute-done.16 = bf16[32,1536]{1,0:T(8,128)(2,1)S(1)} collective-permute-done((bf16[32,1536]{1,0:T(8,128)(2,1)S(1)}, bf16[32,1536]{1,0:T(8,128)(2,1)S(1)}, u32[]{:S(2)}, u32[]{:S(2)}) %collective-permute-start.16) | collective-permute-done | bytes 98336 | tf_op jit(solution)/shard_map/ppermute | solution.py:15
  146.6 4.1 %collective-permute-done.15 = bf16[32,1536]{1,0:T(8,128)(2,1)S(1)} collective-permute-done((bf16[32,1536]{1,0:T(8,128)(2,1)S(1)}, bf16[32,1536]{1,0:T(8,128)(2,1)S(1)}, u32[]{:S(2)}, u32[]{:S(2)}) %collective-permute-start.15) | collective-permute-done | bytes 98336 | tf_op jit(solution)/shard_map/ppermute | solution.py:15
  150.7 1.5 collective-permute-start.17
  152.8 2.1 collective-permute-start.25
  154.9 4.3 %collective-permute-done.17 = bf16[32,1536]{1,0:T(8,128)(2,1)S(1)} collective-permute-done((bf16[32,1536]{1,0:T(8,128)(2,1)S(1)}, bf16[32,1536]{1,0:T(8,128)(2,1)S(1)}, u32[]{:S(2)}, u32[]{:S(2)}) %collective-permute-start.17) | collective-permute-done | bytes 98336 | tf_op jit(solution)/shard_map/ppermute | solution.py:15
  159.9 1.9 collective-permute-start.19
  161.8 1.8 collective-permute-start.18
  163.6 6.2 %collective-permute-done.18 = bf16[64,1536]{1,0:T(8,128)(2,1)S(1)} collective-permute-done((bf16[64,1536]{1,0:T(8,128)(2,1)S(1)}, bf16[64,1536]{1,0:T(8,128)(2,1)S(1)}, u32[]{:S(2)}, u32[]{:S(2)}) %collective-permute-start.18) | collective-permute-done | bytes 196640 | tf_op jit(solution)/shard_map/ppermute | solution.py:15
  169.8 3.0 %collective-permute-start.21 = (bf16[256,1536]{1,0:T(8,128)(2,1)S(1)}, bf16[256,1536]{1,0:T(8,128)(2,1)S(1)}, u32[]{:S(2)}, u32[]{:S(2)}) collective-permute-start(bf16[256,1536]{1,0:T(8,128)(2,1)S(1)} %constant_dynamic-update-slice_fusion), channel_id=1, source_target_pairs={{0,16},{16,0},{1,17},{17,1},{2,18},{18,2},{3,19},{19,3},{4,20},{20... | collective-permute-start | bytes 2359304 | tf_op jit(solution)/shard_map/ppermute | solution.py:15
  174.0 1.6 collective-permute-start.26
  180.6 5.3 %collective-permute-start.24 = (bf16[16,768]{1,0:T(8,128)(2,1)S(1)}, bf16[16,768]{1,0:T(8,128)(2,1)S(1)}, u32[]{:S(2)}, u32[]{:S(2)}) collective-permute-start(bf16[16,768]{1,0:T(8,128)(2,1)S(1)} %get-tuple-element.41), channel_id=1, source_target_pairs={{0,16},{16,32},{32,48},{48,64},{64,80},{80,96},{96,112},{112,128},... | collective-permute-start | bytes 73736 | tf_op jit(solution)/shard_map/ppermute | solution.py:20
  185.9 4.8 %collective-permute-done.27 = bf16[192,768]{1,0:T(8,128)(2,1)S(1)} collective-permute-done((bf16[192,768]{1,0:T(8,128)(2,1)S(1)}, bf16[192,768]{1,0:T(8,128)(2,1)S(1)}, u32[]{:S(2)}, u32[]{:S(2)}) %collective-permute-start.27) | collective-permute-done | bytes 294944 | tf_op jit(solution)/shard_map/ppermute | solution.py:15
  191.6 3.5 %all-to-all-start.1 = ((bf16[4,48,768]{2,1,0:T(8,128)(2,1)}), bf16[4,48,768]{2,1,0:T(8,128)(2,1)S(1)}, u32[]{:S(2)}, u32[]{:S(2)}) async-start(bf16[4,48,768]{2,1,0:T(8,128)(2,1)} %bitcast.41), calls=%async_computation.1 | async-start | bytes 589824 | tf_op jit(solution)/shard_map/all_to_all | solution.py:445
  195.0 3.6 %fusion.8 = f32[256,1536]{1,0:T(8,128)} fusion(bf16[256,768]{1,0:T(8,128)(2,1)S(1)} %fusion.29, bf16[3,1536,768]{2,1,0:T(8,128)(2,1)} %taps_hbm.3), kind=kOutput, calls=%fused_computation.16 | convolution fusion | flops 603979776 | bytes 4325376 | tf_op jit(solution)/shard_map/dot_general | solution.py:45
  198.7 2.9 %collective-permute-start.23 = (bf16[16,768]{1,0:T(8,128)(2,1)S(1)}, bf16[16,768]{1,0:T(8,128)(2,1)S(1)}, u32[]{:S(2)}, u32[]{:S(2)}) collective-permute-start(bf16[16,768]{1,0:T(8,128)(2,1)S(1)} %get-tuple-element.40), channel_id=1, source_target_pairs={{16,0},{32,16},{48,32},{64,48},{80,64},{96,80},{112,96},{128,112},... | collective-permute-start | bytes 73736 | tf_op jit(solution)/shard_map/ppermute | solution.py:21
  201.6 3.7 %fusion.6 = f32[256,1536]{1,0:T(8,128)} fusion(bf16[3,1536,768]{2,1,0:T(8,128)(2,1)} %taps_hbm.3, bf16[256,768]{1,0:T(8,128)(2,1)S(1)} %fusion.29, bf16[16,768]{1,0:T(8,128)(2,1)S(1)} %collective-permute-done.24), kind=kOutput, calls=%fused_computation.14 | convolution fusion | flops 604766208 | bytes 4349952 | tf_op jit(solution)/shard_map/dot_general | solution.py:45
  205.3 2.5 %collective-permute-start.31 = (bf16[48,768]{1,0:T(8,128)(2,1)S(1)}, bf16[48,768]{1,0:T(8,128)(2,1)S(1)}, u32[]{:S(2)}, u32[]{:S(2)}) collective-permute-start(bf16[48,768]{1,0:T(8,128)(2,1)S(1)} %reduce_sum.52), channel_id=1, source_target_pairs={{0,192},{64,0},{128,64},{192,128},{1,193},{65,1},{129,65},{193,129... | collective-permute-start | bytes 221192 | tf_op jit(solution)/shard_map/ppermute | solution.py:15
  207.8 1.5 collective-permute-start.29
  209.3 4.1 %fusion.28 = (f32[256]{0:T(256)S(1)}, f32[256,1536]{1,0:T(8,128)S(1)}) fusion(bf16[256,1536]{1,0:T(8,128)(2,1)S(1)} %bitcast.100, f32[1536]{0:T(1024)S(1)} %copy-done.8, f32[256]{0:T(256)S(1)} %copy-done.10, f32[256,1536]{1,0:T(8,128)} %fusion.6, f32[256,1536]{1,0:T(8,128)} %fusion.8, bf16[3,1536,768]{2,1,0:T(8,128)(2,1)} %taps_hbm.3, ...), kind=kOutput, calls=%fused_computation.39 | convolution fusion | flops 611450624 | bytes 8290304 | tf_op jit(solution)/shard_map/dot_general | solution.py:45
  213.7 2.4 %collective-permute-start.32 = (bf16[48,768]{1,0:T(8,128)(2,1)S(1)}, bf16[48,768]{1,0:T(8,128)(2,1)S(1)}, u32[]{:S(2)}, u32[]{:S(2)}) collective-permute-start(bf16[48,768]{1,0:T(8,128)(2,1)S(1)} %add_convert_fusion.4), channel_id=1, source_target_pairs={{0,32},{32,0},{1,33},{33,1},{2,34},{34,2},{3,35},{35,3},{4,36},{36... | collective-permute-start | bytes 221192 | tf_op jit(solution)/shard_map/ppermute | solution.py:15
  216.2 4.8 %collective-permute-done.32 = bf16[48,768]{1,0:T(8,128)(2,1)S(1)} collective-permute-done((bf16[48,768]{1,0:T(8,128)(2,1)S(1)}, bf16[48,768]{1,0:T(8,128)(2,1)S(1)}, u32[]{:S(2)}, u32[]{:S(2)}) %collective-permute-start.32) | collective-permute-done | bytes 73760 | tf_op jit(solution)/shard_map/ppermute | solution.py:15
  221.0 4.0 %collective-permute-start.33 = (f32[48,768]{1,0:T(8,128)S(1)}, f32[48,768]{1,0:T(8,128)S(1)}, u32[]{:S(2)}, u32[]{:S(2)}) collective-permute-start(f32[48,768]{1,0:T(8,128)S(1)} %convert_add_fusion.3), channel_id=1, source_target_pairs={{0,16},{16,0},{1,17},{17,1},{2,18},{18,2},{3,19},{19,3},{4,20},{20... | collective-permute-start | bytes 442376 | tf_op jit(solution)/shard_map/ppermute | solution.py:15
  (151 shorter events, 41.9 us)
Async XLA Ops:
  0.6 26.8 %copy-start = (bf16[1,256,1536]{2,1,0:T(8,128)(2,1)S(1)}, bf16[1,256,1536]{2,1,0:T(8,128)(2,1)}, u32[]{:S(2)}) copy-start(bf16[1,256,1536]{2,1,0:T(8,128)(2,1)} %param.10) | copy-start | bytes 2359300
  0.6 25.9 %copy-start.7 = (f32[1536]{0:T(1024)S(1)}, f32[1536]{0:T(1024)}, u32[]{:S(2)}) copy-start(f32[1536]{0:T(1024)} %param.11) | copy-start | bytes 18436
  0.7 25.9 %copy-start.6 = (s32[1536]{0:T(1024)S(1)}, s32[1536]{0:T(1024)}, u32[]{:S(2)}) copy-start(s32[1536]{0:T(1024)} %param.15) | copy-start | bytes 18436
  2.6 86.1 %collective-permute-start.12 = (bf16[128,1536]{0,1:T(8,128)(2,1)}, bf16[128,1536]{0,1:T(8,128)(2,1)}, u32[]{:S(2)}, u32[]{:S(2)}) collective-permute-start(bf16[128,1536]{0,1:T(8,128)(2,1)} %select_bitcast_fusion), channel_id=1, source_target_pairs={{0,12},{4,0},{8,4},{12,8},{1,13},{5,1},{9,5},{13,9},{2,14},{6,2},{... | collective-permute-start | bytes 1179656 | tf_op jit(solution)/shard_map/ppermute | solution.py:15
  5.9 82.8 %collective-permute-start.11 = (bf16[128,1536]{0,1:T(8,128)(2,1)}, bf16[128,1536]{0,1:T(8,128)(2,1)}, u32[]{:S(2)}, u32[]{:S(2)}) collective-permute-start(bf16[128,1536]{0,1:T(8,128)(2,1)} %select_bitcast_fusion), channel_id=1, source_target_pairs={{0,8},{4,12},{8,0},{12,4},{1,9},{5,13},{9,1},{13,5},{2,10},{6,14},... | collective-permute-start | bytes 1179656 | tf_op jit(solution)/shard_map/ppermute | solution.py:15
  6.5 82.3 %collective-permute-start.10 = (bf16[128,1536]{0,1:T(8,128)(2,1)}, bf16[128,1536]{0,1:T(8,128)(2,1)}, u32[]{:S(2)}, u32[]{:S(2)}) collective-permute-start(bf16[128,1536]{0,1:T(8,128)(2,1)} %select_bitcast_fusion), channel_id=1, source_target_pairs={{0,4},{4,8},{8,12},{12,0},{1,5},{5,9},{9,13},{13,1},{2,6},{6,10},{... | collective-permute-start | bytes 1179656 | tf_op jit(solution)/shard_map/ppermute | solution.py:15
  7.9 18.8 %collective-permute-start = (bf16[16,1536]{1,0:T(8,128)(2,1)S(1)}, bf16[16,1536]{1,0:T(8,128)(2,1)S(1)}, u32[]{:S(2)}, u32[]{:S(2)}) collective-permute-start(bf16[16,1536]{1,0:T(8,128)(2,1)S(1)} %get-tuple-element.36), channel_id=1, source_target_pairs={{0,16},{16,32},{32,48},{48,64},{64,80},{80,96},{96,112},{112,128},... | collective-permute-start | bytes 147464 | tf_op jit(solution)/shard_map/ppermute | solution.py:20
  18.1 9.3 %collective-permute-start.1 = (bf16[16,1536]{1,0:T(8,128)(2,1)S(1)}, bf16[16,1536]{1,0:T(8,128)(2,1)S(1)}, u32[]{:S(2)}, u32[]{:S(2)}) collective-permute-start(bf16[16,1536]{1,0:T(8,128)(2,1)S(1)} %get-tuple-element.37), channel_id=1, source_target_pairs={{16,0},{32,16},{48,32},{64,48},{80,64},{96,80},{112,96},{128,112},... | collective-permute-start | bytes 147464 | tf_op jit(solution)/shard_map/ppermute | solution.py:21
  27.4 11.5 %copy-start.4 = (f32[1,4,4096]{2,1,0:T(4,128)S(1)}, f32[1,4,4096]{2,1,0:T(4,128)}, u32[]{:S(2)}) copy-start(f32[1,4,4096]{2,1,0:T(4,128)} %param.19) | copy-start | bytes 196612
  39.0 9.8 %copy-start.13 = (s32[1,64]{1,0:T(1,128)S(1)}, s32[1,64]{1,0:T(1,128)}, u32[]{:S(2)}) copy-start(s32[1,64]{1,0:T(1,128)} %param.18) | copy-start | bytes 772
  39.0 10.4 %copy-start.11 = (s32[1,64]{1,0:T(1,128)S(1)}, s32[1,64]{1,0:T(1,128)}, u32[]{:S(2)}) copy-start(s32[1,64]{1,0:T(1,128)} %param.17) | copy-start | bytes 772
  41.4 30.5 %copy-start.2 = (bf16[256,2304]{1,0:T(8,128)(2,1)S(1)}, bf16[256,2304]{1,0:T(8,128)(2,1)}, u32[]{:S(2)}) copy-start(bf16[256,2304]{1,0:T(8,128)(2,1)} %copy-done.1) | copy-start | bytes 3538948
  41.4 55.3 %collective-permute-start.22 = (bf16[288,1536]{1,0:T(8,128)(2,1)}, bf16[288,1536]{1,0:T(8,128)(2,1)}, u32[]{:S(2)}, u32[]{:S(2)}) collective-permute-start(bf16[288,1536]{1,0:T(8,128)(2,1)} %pad_maximum_fusion.1), channel_id=1, source_target_pairs={{0,240},{16,224},{32,208},{48,192},{64,176},{80,160},{96,144},{112... | collective-permute-start | bytes 2654216 | tf_op jit(solution)/shard_map/ppermute | solution.py:359
  67.9 19.8 %all-to-all-start = ((f32[4,4,1152]{2,1,0:T(4,128)}), f32[4,4,1152]{2,1,0:T(4,128)}, u32[]{:S(2)}, u32[]{:S(2)}) async-start(f32[4,4,1152]{2,1,0:T(4,128)} %pad_maximum_fusion.12), calls=%async_computation | async-start | bytes 147456 | tf_op jit(solution)/shard_map/all_to_all | solution.py:308
  71.8 18.5 %collective-permute-start.2 = (bf16[256,2304]{1,0:T(8,128)(2,1)S(1)}, bf16[256,2304]{1,0:T(8,128)(2,1)}, u32[]{:S(2)}, u32[]{:S(2)}) collective-permute-start(bf16[256,2304]{1,0:T(8,128)(2,1)S(1)} %copy-done.2), channel_id=1, source_target_pairs={{0,16},{16,0},{1,17},{17,1},{2,18},{18,2},{3,19},{19,3},{4,20},{20... | collective-permute-start | bytes 3538952 | tf_op jit(solution)/shard_map/ppermute | solution.py:15
  90.3 46.7 %collective-permute-start.13 = (bf16[512,1536]{0,1:T(8,128)(2,1)S(1)}, bf16[512,1536]{0,1:T(8,128)(2,1)S(1)}, u32[]{:S(2)}, u32[]{:S(2)}) collective-permute-start(bf16[512,1536]{0,1:T(8,128)(2,1)S(1)} %pad_maximum_fusion), channel_id=1, source_target_pairs={{0,16},{16,0},{1,17},{17,1},{2,18},{18,2},{3,19},{19,3},{4,20},{20... | collective-permute-start | bytes 4718600 | tf_op jit(solution)/shard_map/ppermute | solution.py:15
  91.9 4.7 %copy-start.3 = (bf16[256,1536]{1,0:T(8,128)(2,1)S(1)}, bf16[256,1536]{1,0:T(8,128)(2,1)}, u32[]{:S(2)}) copy-start(bf16[256,1536]{1,0:T(8,128)(2,1)} %get-tuple-element.14.own_ref) | copy-start | bytes 2359300
  92.0 17.0 %collective-permute-start.3 = (bf16[64,2304]{1,0:T(8,128)(2,1)S(1)}, bf16[64,2304]{1,0:T(8,128)(2,1)S(1)}, u32[]{:S(2)}, u32[]{:S(2)}) collective-permute-start(bf16[64,2304]{1,0:T(8,128)(2,1)S(1)} %get-tuple-element.31), channel_id=1, source_target_pairs={{0,64},{64,128},{128,192},{192,0},{1,65},{65,129},{129,193},{193,1... | collective-permute-start | bytes 884744 | tf_op jit(solution)/shard_map/ppermute | solution.py:15
  94.4 14.6 %collective-permute-start.5 = (bf16[64,2304]{1,0:T(8,128)(2,1)S(1)}, bf16[64,2304]{1,0:T(8,128)(2,1)S(1)}, u32[]{:S(2)}, u32[]{:S(2)}) collective-permute-start(bf16[64,2304]{1,0:T(8,128)(2,1)S(1)} %get-tuple-element.32), channel_id=1, source_target_pairs={{0,192},{64,0},{128,64},{192,128},{1,193},{65,1},{129,65},{193,129... | collective-permute-start | bytes 884744 | tf_op jit(solution)/shard_map/ppermute | solution.py:15
  94.8 14.2 %collective-permute-start.4 = (bf16[64,2304]{1,0:T(8,128)(2,1)S(1)}, bf16[64,2304]{1,0:T(8,128)(2,1)S(1)}, u32[]{:S(2)}, u32[]{:S(2)}) collective-permute-start(bf16[64,2304]{1,0:T(8,128)(2,1)S(1)} %get-tuple-element.33), channel_id=1, source_target_pairs={{0,128},{64,192},{128,0},{192,64},{1,129},{65,193},{129,1},{193,65... | collective-permute-start | bytes 884744 | tf_op jit(solution)/shard_map/ppermute | solution.py:15
  109.2 11.1 %collective-permute-start.6 = (bf16[32,2304]{1,0:T(8,128)(2,1)S(1)}, bf16[32,2304]{1,0:T(8,128)(2,1)S(1)}, u32[]{:S(2)}, u32[]{:S(2)}) collective-permute-start(bf16[32,2304]{1,0:T(8,128)(2,1)S(1)} %dynamic-slice_bitcast_fusion.6), channel_id=1, source_target_pairs={{0,32},{32,0},{1,33},{33,1},{2,34},{34,2},{3,35},{35,3},{4,36},{36... | collective-permute-start | bytes 442376 | tf_op jit(solution)/shard_map/ppermute | solution.py:15
  120.3 6.3 %collective-permute-start.9 = (bf16[32,2304]{1,0:T(8,128)(2,1)S(1)}, bf16[32,2304]{1,0:T(8,128)(2,1)S(1)}, u32[]{:S(2)}, u32[]{:S(2)}) collective-permute-start(bf16[32,2304]{1,0:T(8,128)(2,1)S(1)} %fusion.51), channel_id=1, source_target_pairs={{0,3},{1,0},{2,1},{3,2},{4,7},{5,4},{6,5},{7,6},{8,11},{9,8},{10,9... | collective-permute-start | bytes 442376 | tf_op jit(solution)/shard_map/ppermute | solution.py:15
  124.5 12.0 %collective-permute-start.8 = (bf16[32,2304]{1,0:T(8,128)(2,1)S(1)}, bf16[32,2304]{1,0:T(8,128)(2,1)S(1)}, u32[]{:S(2)}, u32[]{:S(2)}) collective-permute-start(bf16[32,2304]{1,0:T(8,128)(2,1)S(1)} %fusion.51), channel_id=1, source_target_pairs={{0,2},{1,3},{2,0},{3,1},{4,6},{5,7},{6,4},{7,5},{8,10},{9,11},{10,... | collective-permute-start | bytes 442376 | tf_op jit(solution)/shard_map/ppermute | solution.py:15
  124.5 12.0 %collective-permute-start.7 = (bf16[32,2304]{1,0:T(8,128)(2,1)S(1)}, bf16[32,2304]{1,0:T(8,128)(2,1)S(1)}, u32[]{:S(2)}, u32[]{:S(2)}) collective-permute-start(bf16[32,2304]{1,0:T(8,128)(2,1)S(1)} %fusion.51), channel_id=1, source_target_pairs={{0,1},{1,2},{2,3},{3,0},{4,5},{5,6},{6,7},{7,4},{8,9},{9,10},{10,1... | collective-permute-start | bytes 442376 | tf_op jit(solution)/shard_map/ppermute | solution.py:15
  139.3 4.7 %collective-permute-start.14 = (bf16[32,1536]{1,0:T(8,128)(2,1)S(1)}, bf16[32,1536]{1,0:T(8,128)(2,1)S(1)}, u32[]{:S(2)}, u32[]{:S(2)}) collective-permute-start(bf16[32,1536]{1,0:T(8,128)(2,1)S(1)} %get-tuple-element.42), channel_id=1, source_target_pairs={{0,3},{1,0},{2,1},{3,2},{4,7},{5,4},{6,5},{7,6},{8,11},{9,8},{10,9... | collective-permute-start | bytes 294920 | tf_op jit(solution)/shard_map/ppermute | solution.py:15
  139.7 6.9 %collective-permute-start.16 = (bf16[32,1536]{1,0:T(8,128)(2,1)S(1)}, bf16[32,1536]{1,0:T(8,128)(2,1)S(1)}, u32[]{:S(2)}, u32[]{:S(2)}) collective-permute-start(bf16[32,1536]{1,0:T(8,128)(2,1)S(1)} %get-tuple-element.43), channel_id=1, source_target_pairs={{0,1},{1,2},{2,3},{3,0},{4,5},{5,6},{6,7},{7,4},{8,9},{9,10},{10,1... | collective-permute-start | bytes 294920 | tf_op jit(solution)/shard_map/ppermute | solution.py:15
  140.9 9.8 %collective-permute-start.15 = (bf16[32,1536]{1,0:T(8,128)(2,1)S(1)}, bf16[32,1536]{1,0:T(8,128)(2,1)S(1)}, u32[]{:S(2)}, u32[]{:S(2)}) collective-permute-start(bf16[32,1536]{1,0:T(8,128)(2,1)S(1)} %get-tuple-element.44), channel_id=1, source_target_pairs={{0,2},{1,3},{2,0},{3,1},{4,6},{5,7},{6,4},{7,5},{8,10},{9,11},{10,... | collective-permute-start | bytes 294920 | tf_op jit(solution)/shard_map/ppermute | solution.py:15
  150.7 8.5 %collective-permute-start.17 = (bf16[32,1536]{1,0:T(8,128)(2,1)S(1)}, bf16[32,1536]{1,0:T(8,128)(2,1)S(1)}, u32[]{:S(2)}, u32[]{:S(2)}) collective-permute-start(bf16[32,1536]{1,0:T(8,128)(2,1)S(1)} %get-tuple-element.27), channel_id=1, source_target_pairs={{0,32},{32,0},{1,33},{33,1},{2,34},{34,2},{3,35},{35,3},{4,36},{36... | collective-permute-start | bytes 294920 | tf_op jit(solution)/shard_map/ppermute | solution.py:15
  152.8 20.5 %collective-permute-start.25 = (bf16[768,768]{1,0:T(8,128)(2,1)S(1)}, bf16[768,768]{1,0:T(8,128)(2,1)S(1)}, u32[]{:S(2)}, u32[]{:S(2)}) collective-permute-start(bf16[768,768]{1,0:T(8,128)(2,1)S(1)} %add_convert_fusion.1), channel_id=1, source_target_pairs={{0,16},{16,0},{1,17},{17,1},{2,18},{18,2},{3,19},{19,3},{4,20},{20... | collective-permute-start | bytes 3538952 | tf_op jit(solution)/shard_map/ppermute | solution.py:15
  159.3 10.5 %collective-permute-start.20 = (bf16[64,1536]{1,0:T(8,128)(2,1)S(1)}, bf16[64,1536]{1,0:T(8,128)(2,1)S(1)}, u32[]{:S(2)}, u32[]{:S(2)}) collective-permute-start(bf16[64,1536]{1,0:T(8,128)(2,1)S(1)} %pad_maximum_fusion.10), channel_id=1, source_target_pairs={{0,64},{64,128},{128,192},{192,0},{1,65},{65,129},{129,193},{193,1... | collective-permute-start | bytes 589832 | tf_op jit(solution)/shard_map/ppermute | solution.py:15
  159.9 9.9 %collective-permute-start.19 = (bf16[64,1536]{1,0:T(8,128)(2,1)S(1)}, bf16[64,1536]{1,0:T(8,128)(2,1)S(1)}, u32[]{:S(2)}, u32[]{:S(2)}) collective-permute-start(bf16[64,1536]{1,0:T(8,128)(2,1)S(1)} %pad_maximum_fusion.10), channel_id=1, source_target_pairs={{0,128},{64,192},{128,0},{192,64},{1,129},{65,193},{129,1},{193,65... | collective-permute-start | bytes 589832 | tf_op jit(solution)/shard_map/ppermute | solution.py:15
  161.8 7.9 %collective-permute-start.18 = (bf16[64,1536]{1,0:T(8,128)(2,1)S(1)}, bf16[64,1536]{1,0:T(8,128)(2,1)S(1)}, u32[]{:S(2)}, u32[]{:S(2)}) collective-permute-start(bf16[64,1536]{1,0:T(8,128)(2,1)S(1)} %pad_maximum_fusion.10), channel_id=1, source_target_pairs={{0,192},{64,0},{128,64},{192,128},{1,193},{65,1},{129,65},{193,129... | collective-permute-start | bytes 589832 | tf_op jit(solution)/shard_map/ppermute | solution.py:15
  169.8 7.6 %collective-permute-start.21 = (bf16[256,1536]{1,0:T(8,128)(2,1)S(1)}, bf16[256,1536]{1,0:T(8,128)(2,1)S(1)}, u32[]{:S(2)}, u32[]{:S(2)}) collective-permute-start(bf16[256,1536]{1,0:T(8,128)(2,1)S(1)} %constant_dynamic-update-slice_fusion), channel_id=1, source_target_pairs={{0,16},{16,0},{1,17},{17,1},{2,18},{18,2},{3,19},{19,3},{4,20},{20... | collective-permute-start | bytes 2359304 | tf_op jit(solution)/shard_map/ppermute | solution.py:15
  173.9 3.5 %copy-start.5 = (pred[256,512]{1,0:T(32,128)(4,1)S(1)}, pred[256,512]{1,0:T(32,128)(4,1)}, u32[]{:S(2)}) copy-start(pred[256,512]{1,0:T(32,128)(4,1)} %broadcast_compare_fusion) | copy-start | bytes 393220
  174.0 11.9 %collective-permute-start.26 = (bf16[192,768]{1,0:T(8,128)(2,1)S(1)}, bf16[192,768]{1,0:T(8,128)(2,1)S(1)}, u32[]{:S(2)}, u32[]{:S(2)}) collective-permute-start(bf16[192,768]{1,0:T(8,128)(2,1)S(1)} %get-tuple-element.28), channel_id=1, source_target_pairs={{0,4},{4,8},{8,12},{12,0},{1,5},{5,9},{9,13},{13,1},{2,6},{6,10},{... | collective-permute-start | bytes 884744 | tf_op jit(solution)/shard_map/ppermute | solution.py:15
  175.6 10.3 %collective-permute-start.28 = (bf16[192,768]{1,0:T(8,128)(2,1)S(1)}, bf16[192,768]{1,0:T(8,128)(2,1)S(1)}, u32[]{:S(2)}, u32[]{:S(2)}) collective-permute-start(bf16[192,768]{1,0:T(8,128)(2,1)S(1)} %get-tuple-element.29), channel_id=1, source_target_pairs={{0,12},{4,0},{8,4},{12,8},{1,13},{5,1},{9,5},{13,9},{2,14},{6,2},{... | collective-permute-start | bytes 884744 | tf_op jit(solution)/shard_map/ppermute | solution.py:15
  176.7 14.0 %collective-permute-start.27 = (bf16[192,768]{1,0:T(8,128)(2,1)S(1)}, bf16[192,768]{1,0:T(8,128)(2,1)S(1)}, u32[]{:S(2)}, u32[]{:S(2)}) collective-permute-start(bf16[192,768]{1,0:T(8,128)(2,1)S(1)} %get-tuple-element.30), channel_id=1, source_target_pairs={{0,8},{4,12},{8,0},{12,4},{1,9},{5,13},{9,1},{13,5},{2,10},{6,14},... | collective-permute-start | bytes 884744 | tf_op jit(solution)/shard_map/ppermute | solution.py:15
  180.6 21.0 %collective-permute-start.24 = (bf16[16,768]{1,0:T(8,128)(2,1)S(1)}, bf16[16,768]{1,0:T(8,128)(2,1)S(1)}, u32[]{:S(2)}, u32[]{:S(2)}) collective-permute-start(bf16[16,768]{1,0:T(8,128)(2,1)S(1)} %get-tuple-element.41), channel_id=1, source_target_pairs={{0,16},{16,32},{32,48},{48,64},{64,80},{80,96},{96,112},{112,128},... | collective-permute-start | bytes 73736 | tf_op jit(solution)/shard_map/ppermute | solution.py:20
  191.6 13.7 %all-to-all-start.1 = ((bf16[4,48,768]{2,1,0:T(8,128)(2,1)}), bf16[4,48,768]{2,1,0:T(8,128)(2,1)S(1)}, u32[]{:S(2)}, u32[]{:S(2)}) async-start(bf16[4,48,768]{2,1,0:T(8,128)(2,1)} %bitcast.41), calls=%async_computation.1 | async-start | bytes 589824 | tf_op jit(solution)/shard_map/all_to_all | solution.py:445
  198.7 10.6 %copy-start.8 = (f32[1536]{0:T(1024)S(1)}, f32[1536]{0:T(1024)}, u32[]{:S(2)}) copy-start(f32[1536]{0:T(1024)} %param.11) | copy-start | bytes 18436
  198.7 10.6 %copy-start.10 = (f32[256]{0:T(256)S(1)}, f32[256]{0:T(256)}, u32[]{:S(2)}) copy-start(f32[256]{0:T(256)} %get-tuple-element.60) | copy-start | bytes 3076
  198.7 10.6 %collective-permute-start.23 = (bf16[16,768]{1,0:T(8,128)(2,1)S(1)}, bf16[16,768]{1,0:T(8,128)(2,1)S(1)}, u32[]{:S(2)}, u32[]{:S(2)}) collective-permute-start(bf16[16,768]{1,0:T(8,128)(2,1)S(1)} %get-tuple-element.40), channel_id=1, source_target_pairs={{16,0},{32,16},{48,32},{64,48},{80,64},{96,80},{112,96},{128,112},... | collective-permute-start | bytes 73736 | tf_op jit(solution)/shard_map/ppermute | solution.py:21
  205.3 8.1 %collective-permute-start.31 = (bf16[48,768]{1,0:T(8,128)(2,1)S(1)}, bf16[48,768]{1,0:T(8,128)(2,1)S(1)}, u32[]{:S(2)}, u32[]{:S(2)}) collective-permute-start(bf16[48,768]{1,0:T(8,128)(2,1)S(1)} %reduce_sum.52), channel_id=1, source_target_pairs={{0,192},{64,0},{128,64},{192,128},{1,193},{65,1},{129,65},{193,129... | collective-permute-start | bytes 221192 | tf_op jit(solution)/shard_map/ppermute | solution.py:15
  207.8 5.9 %collective-permute-start.30 = (bf16[48,768]{1,0:T(8,128)(2,1)S(1)}, bf16[48,768]{1,0:T(8,128)(2,1)S(1)}, u32[]{:S(2)}, u32[]{:S(2)}) collective-permute-start(bf16[48,768]{1,0:T(8,128)(2,1)S(1)} %reduce_sum.52), channel_id=1, source_target_pairs={{0,64},{64,128},{128,192},{192,0},{1,65},{65,129},{129,193},{193,1... | collective-permute-start | bytes 221192 | tf_op jit(solution)/shard_map/ppermute | solution.py:15
  207.8 5.9 %collective-permute-start.29 = (bf16[48,768]{1,0:T(8,128)(2,1)S(1)}, bf16[48,768]{1,0:T(8,128)(2,1)S(1)}, u32[]{:S(2)}, u32[]{:S(2)}) collective-permute-start(bf16[48,768]{1,0:T(8,128)(2,1)S(1)} %reduce_sum.52), channel_id=1, source_target_pairs={{0,128},{64,192},{128,0},{192,64},{1,129},{65,193},{129,1},{193,65... | collective-permute-start | bytes 221192 | tf_op jit(solution)/shard_map/ppermute | solution.py:15
  209.3 15.7 %copy-start.9 = (f32[256]{0:T(256)S(1)}, f32[256]{0:T(256)}, u32[]{:S(2)}) copy-start(f32[256]{0:T(256)} %get-tuple-element.59) | copy-start | bytes 3076
  213.7 7.2 %collective-permute-start.32 = (bf16[48,768]{1,0:T(8,128)(2,1)S(1)}, bf16[48,768]{1,0:T(8,128)(2,1)S(1)}, u32[]{:S(2)}, u32[]{:S(2)}) collective-permute-start(bf16[48,768]{1,0:T(8,128)(2,1)S(1)} %add_convert_fusion.4), channel_id=1, source_target_pairs={{0,32},{32,0},{1,33},{33,1},{2,34},{34,2},{3,35},{35,3},{4,36},{36... | collective-permute-start | bytes 221192 | tf_op jit(solution)/shard_map/ppermute | solution.py:15
  221.0 5.3 %collective-permute-start.33 = (f32[48,768]{1,0:T(8,128)S(1)}, f32[48,768]{1,0:T(8,128)S(1)}, u32[]{:S(2)}, u32[]{:S(2)}) collective-permute-start(f32[48,768]{1,0:T(8,128)S(1)} %convert_add_fusion.3), channel_id=1, source_target_pairs={{0,16},{16,0},{1,17},{17,1},{2,18},{18,2},{3,19},{19,3},{4,20},{20... | collective-permute-start | bytes 442376 | tf_op jit(solution)/shard_map/ppermute | solution.py:15
  (3 other events, 4.6 us)
where the time goes:
time: 228 us; the launch traced here: 227 us
  starting transfers between devices  81.3 us (36%)
  waiting for transfers between devices  59.7 us (26%)
  other arithmetic  25.3 us (11%)
  Pallas kernels  22.8 us (10%)
  local copies, waits for them, and re-layouts  19.3 us (8%)
  matrix products  17.1 us (8%)
    ppermute x29, starting transfers between devices, shifted(): lax.ppermute(block, axis, [(i, (i + shift) % count) for i in range(count)])  46.3 us
    ppermute x29, waiting for transfers between devices, shifted(): lax.ppermute(block, axis, [(i, (i + shift) % count) for i in range(count)])  45.9 us
    dot_general x14, matrix products, dot(): lax.dot_general(left, right, (((over[0],), (over[1],)), ((), ())), prefer...  17.1 us
    ppermute x2, starting transfers between devices, edge_rows(): lax.ppermute(block[-width:], BINS, [(i, i + 1) for i in range(count - 1)])  15.5 us
    all_to_all x1, waiting for transfers between devices, deal_targets(): parts = lax.all_to_all(parts, 'zl', split_axis=0, concat_axis=0, tiled=True)  13 us
    pallas_call x1, Pallas kernels, reflect(): pl.pallas_call(reflect_kernel, out_shape=[jax.ShapeDtypeStruct((count, ch...  12.3 us
    pallas_call x1, Pallas kernels, forward(): pl.pallas_call(forward_kernel, out_shape=[payload, payload, jax.ShapeDtyp...  10.5 us
    ppermute x1, starting transfers between devices, whole_step(): lax.ppermute(jnp.concatenate([edges, rows], axis=0), BINS, [(i, bin_devic...  7.37 us
  transfers between devices with their start and end apart: 36, of which 12 were waited for; matrix products, arithmetic and copies ran while one was open for 24% of the time, Pallas kernels for 10%

commit v1 on v0

--- a/solution.py
+++ b/solution.py
@@ -283,30 +283,25 @@
 
 
 def gather_head(head_weight):
-    core = lax.axis_index("core")
-    half = head_weight.shape[1] // 2
-    mine = jnp.where(core == 0, head_weight[:, :half], head_weight[:, half:]).T
+    mine = head_weight.T
     pieces = [shifted(mine, "x", k) for k in range(1, lax.axis_size("x"))]
-    held = jnp.concatenate([mine] + pieces, axis=0)
-    return held, shifted(held, "core", 1)
-
-
-def deal_targets(gene_target, own_strand, own_count):
+    return jnp.concatenate([mine] + pieces, axis=0)
+
+
+def target_rows(gene_target, own_strand, own_count, columns):
     nx, nz = lax.axis_size("x"), lax.axis_size("zl")
-    x, zl, core = (lax.axis_index(a) for a in ("x", "zl", "core"))
+    x = lax.axis_index("x")
     genes, tracks = gene_target.shape
     odd = (lax.broadcasted_iota(jnp.int32, gene_target.shape, 1) & 1) == 1
     swapped = jnp.where(odd, jnp.roll(gene_target, 1, axis=1), jnp.roll(gene_target, -1, axis=1))
     flipped = jnp.where(own_strand[:, None] == 1, swapped, gene_target)
-    parts = flipped.reshape(genes, nx, nz, 2, tracks // (nx * nz * 2))
-    parts = jnp.transpose(parts, (1, 2, 0, 3, 4))
-    parts = jnp.where(core == 0, parts, parts[:, :, :, ::-1])
-    parts = jnp.stack([pick(parts, (x - k) % nx) for k in range(nx)], axis=3)
-    parts = parts.reshape(nz, genes, tracks // nz)
-    counts = jnp.broadcast_to(wide(own_count)[None, :, None], (nz, genes, 128))
-    parts = jnp.concatenate([parts, counts], axis=2)
-    parts = lax.all_to_all(parts, "zl", split_axis=0, concat_axis=0, tiled=True)
-    return jnp.concatenate([pick(parts, (zl - k) % nz) for k in range(nz)], axis=0)
+    parts = flipped.reshape(genes, nx, nz, tracks // (nx * nz))
+    parts = jnp.transpose(parts, (1, 2, 0, 3))
+    parts = jnp.concatenate([pick(parts, (x - k) % nx) for k in range(nx)], axis=2)
+    rounded = lax.reduce_precision(parts, 8, 7)
+    rest = columns - 2 * parts.shape[2]
+    counts = jnp.broadcast_to(wide(own_count)[None, :, None], (nz, genes, rest))
+    return narrow(jnp.concatenate([rounded, parts - rounded, counts], axis=2))
 
 
 def listed_bins(exon_bins, exon_count):
@@ -346,13 +341,13 @@
     gene_target,
 ):
     ny, nh, nc, nx, nz = (lax.axis_size(a) for a in ("y", "zh", "core", "x", "zl"))
-    y, zh, core, x, _ = (lax.axis_index(a) for a in ("y", "zh", "core", "x", "zl"))
+    y, zh, core, x, zl = (lax.axis_index(a) for a in ("y", "zh", "core", "x", "zl"))
     bin_devices = ny * nh * nc
     bin_index = (y * nh + zh) * nc + core
     rows = features[0]
     count_of_rows, channels = rows.shape
     low, high = edge_rows(rows, DILATION_STEP)
-    head, head_other = gather_head(head_weight)
+    head = gather_head(head_weight)
     entry_bins = listed_bins(exon_bins[0], exon_count[0])
     entries = entry_bins.size
     edges = jnp.concatenate([low, high], axis=0)
@@ -378,10 +373,6 @@
     sent = sent.reshape(nh, -1, kept.shape[1])
     piece = shifted(pick(sent, 1 - zh), "zh", 1)
     sent = narrow(wide(pick(sent, zh)) + wide(piece))
-    gathered = jnp.concatenate([sent] + [shifted(sent, "zl", k) for k in range(1, nz)], axis=0)
-    gathered_active = gathered[:, channels:]
-    gathered = gathered[:, :channels]
-
     distant_bins = by_distance(after(entry_bins, block_out))
     positions = bin_index * count_of_rows + lax.iota(jnp.int32, count_of_rows)
     pick_rows = narrow(distant_bins[None, :] == positions[:, None])
@@ -389,7 +380,17 @@
     gene_strand, exon_count = after((gene_strand, exon_count), block_out)
     own_strand = lax.dynamic_slice_in_dim(gene_strand[0], bin_index * own_genes, own_genes, 0)
     own_count = lax.dynamic_slice_in_dim(exon_count[0], bin_index * own_genes, own_genes, 0)
-    targets = deal_targets(after(gene_target[0], block_out), own_strand, own_count)
+    target = target_rows(
+        after(gene_target[0], block_out), own_strand, own_count, kept.shape[1]
+    )
+    pieces = [jnp.concatenate([sent, pick(target, zl)], axis=0)]
+    for k in range(1, nz):
+        piece = jnp.concatenate([sent, pick(target, (zl + k) % nz)], axis=0)
+        pieces.append(shifted(piece, "zl", k))
+    sent_rows = sent.shape[0]
+    gathered = jnp.concatenate([piece[:sent_rows, :channels] for piece in pieces], axis=0)
+    gathered_active = jnp.concatenate([piece[:sent_rows, channels:] for piece in pieces], axis=0)
+    targets = wide(jnp.concatenate([piece[sent_rows:] for piece in pieces], axis=0))
     rc_grad, rc_narrow = reflect(
         partner,
         norm_gain,
@@ -399,21 +400,18 @@
         out_weight,
     )
 
-    logits = jnp.concatenate([dot(gathered, head, (1, 1)), dot(gathered, head_other, (1, 1))], axis=1)
-    grouped = (nz * own_genes, exon_bins.shape[2], logits.shape[1])
+    logits = dot(gathered, head, (1, 1))
     tracks = logits.shape[1]
+    grouped = (nz * own_genes, exon_bins.shape[2], tracks)
     predicted = narrow(jax.nn.softplus(logits)).reshape(grouped)
-    counted = lax.broadcasted_iota(jnp.int32, grouped[:2], 1) < targets[:, tracks:tracks + 1].astype(
-        jnp.int32
-    )
+    counted = lax.broadcasted_iota(jnp.int32, grouped[:2], 1) < targets[:, -1:].astype(jnp.int32)
     coverage = jnp.sum(jnp.where(counted[:, :, None], wide(predicted), 0.0), axis=1)
-    spread_back = narrow(1.0 - targets[:, :tracks] / (1.0 + coverage))
+    wanted = targets[:, :tracks] + targets[:, tracks : 2 * tracks]
+    spread_back = narrow(1.0 - wanted / (1.0 + coverage))
     logit_grad = narrow(
         wide(spread_back)[:, None, :] * jax.nn.sigmoid(logits).reshape(grouped)
     ).reshape(logits.shape)
-    entry_grad = narrow(
-        dot(logit_grad[:, : tracks // 2], head) + dot(logit_grad[:, tracks // 2 :], head_other)
-    )
+    entry_grad = narrow(dot(logit_grad, head))
     back = entry_grad.reshape(nz, -1, channels)
     pieces = [shifted(back[k], "zl", -k) for k in range(1, nz)]
     back = narrow(wide(back[0]) + sum(wide(piece) for piece in pieces))
@@ -442,8 +440,8 @@
     pieces = [shifted(pick(share, (x + k) % nx), "x", k) for k in range(1, nx)]
     share = wide(pick(share, x)) + sum(wide(piece) for piece in pieces)
     share = narrow(share).reshape(nz, -1, half)
-    pieces = lax.all_to_all(share, "zl", split_axis=0, concat_axis=0, tiled=True)
-    share = narrow(jnp.sum(wide(pieces), axis=0))
+    pieces = [shifted(pick(share, (zl + k) % nz), "zl", k) for k in range(1, nz)]
+    share = narrow(wide(pick(share, zl)) + sum(wide(piece) for piece in pieces))
     share = narrow(
         (wide(share) + wide(shifted(share, "y", 2)))
         + (wide(shifted(share, "y", 1)) + wide(shifted(share, "y", 3)))

time: 228 us -> 235 us (1.031)
  waiting for transfers between devices: 59.7 us -> 76.3 us
  starting transfers between devices: 81.3 us -> 95.8 us
  other arithmetic: 25.3 us -> 13.9 us
  local copies, waits for them, and re-layouts: 19.3 us -> 13 us
  matrix products: 17.1 us -> 11.8 us
    ppermute x1, waiting for transfers between devices: 0.01 us -> 29.4 us  [whole_step(): lax.ppermute(jnp.concatenate([edges, rows], axis=0), BINS, [(i, bin_devic...]
    ppermute x29 -> x31, starting transfers between devices: 46.3 us -> 60.1 us  [shifted(): lax.ppermute(block, axis, [(i, (i + shift) % count) for i in range(count)])]
    all_to_all x2 -> x0, waiting for transfers between devices: 13 us -> none  [the longest x1 13 us: deal_targets(): parts = lax.all_to_all(parts, 'zl', split_axis=0, concat_axis=0, tiled=True)]
    all_to_all x2 -> x0, starting transfers between devices: 7.35 us -> none  [the longest x1 3.9 us: deal_targets(): parts = lax.all_to_all(parts, 'zl', split_axis=0, concat_axis=0, tiled=True)]
    ppermute x1, starting transfers between devices: 7.37 us -> 14.3 us  [whole_step(): lax.ppermute(jnp.concatenate([edges, rows], axis=0), BINS, [(i, bin_devic...]
    dot_general x14 -> x12, matrix products: 17.1 us -> 11.8 us  [dot(): lax.dot_general(left, right, (((over[0],), (over[1],)), ((), ())), prefer...]
    reshape x3 -> x0, local copies, waits for them, and re-layouts: 4.53 us -> none  [the longest x2 3.02 us: deal_targets(): parts = flipped.reshape(genes, nx, nz, 2, tracks // (nx * nz * 2))]
    concatenate x4 -> x2, other arithmetic: 3.08 us -> 0.08 us  [the longest x1 0.04 us: whole_step(): piece = jnp.concatenate([sent, pick(target, (zl + k) % nz)], axis=0)]
  transfers between devices with their start and end apart: 36 -> 36, of which waited for: 12 -> 14; matrix products, arithmetic and copies ran while one was open for 24% -> 12% of each run, Pallas kernels for 10% -> 9%
where the time goes in v1:
time: 235 us; the launch traced here: 234 us
  starting transfers between devices  95.8 us (41%)
  waiting for transfers between devices  76.3 us (32%)
  Pallas kernels  21.6 us (9%)
  other arithmetic  13.9 us (6%)
  local copies, waits for them, and re-layouts  13 us (6%)
  matrix products  11.8 us (5%)
    ppermute x31, starting transfers between devices, shifted(): lax.ppermute(block, axis, [(i, (i + shift) % count) for i in range(count)])  60.1 us
    ppermute x31, waiting for transfers between devices, shifted(): lax.ppermute(block, axis, [(i, (i + shift) % count) for i in range(count)])  46.8 us
    ppermute x1, waiting for transfers between devices, whole_step(): lax.ppermute(jnp.concatenate([edges, rows], axis=0), BINS, [(i, bin_devic...  29.4 us
    ppermute x2, starting transfers between devices, edge_rows(): lax.ppermute(block[-width:], BINS, [(i, i + 1) for i in range(count - 1)])  16.6 us
    ppermute x1, starting transfers between devices, whole_step(): lax.ppermute(jnp.concatenate([edges, rows], axis=0), BINS, [(i, bin_devic...  14.3 us
    dot_general x12, matrix products, dot(): lax.dot_general(left, right, (((over[0],), (over[1],)), ((), ())), prefer...  11.8 us
    pallas_call x1, Pallas kernels, reflect(): pl.pallas_call(reflect_kernel, out_shape=[jax.ShapeDtypeStruct((count, ch...  11.1 us
    pallas_call x1, Pallas kernels, forward(): pl.pallas_call(forward_kernel, out_shape=[payload, payload, jax.ShapeDtyp...  10.5 us
  transfers between devices with their start and end apart: 36, of which 14 were waited for; matrix products, arithmetic and copies ran while one was open for 12% of the time, Pallas kernels for 9%

profile of v1, /device:TPU:1, one launch (start us, length us, event | category | flops | bytes accessed | tf_op | source)
XLA Modules:
  0.0 234.0 jit_solution(6716396088112714275)
XLA Ops:
  0.6 3.4 %collective-permute-start.12 = (bf16[256,1536]{0,1:T(8,128)(2,1)}, bf16[256,1536]{0,1:T(8,128)(2,1)}, u32[]{:S(2)}, u32[]{:S(2)}) collective-permute-start(bf16[256,1536]{0,1:T(8,128)(2,1)} %bitcast.132), channel_id=1, source_target_pairs={{0,12},{4,0},{8,4},{12,8},{1,13},{5,1},{9,5},{13,9},{2,14},{6,2},{... | collective-permute-start | bytes 2359304 | tf_op jit(solution)/shard_map/ppermute | solution.py:15
  5.4 9.9 %collective-permute-start = (bf16[16,1536]{1,0:T(8,128)(2,1)S(1)}, bf16[16,1536]{1,0:T(8,128)(2,1)S(1)}, u32[]{:S(2)}, u32[]{:S(2)}) collective-permute-start(bf16[16,1536]{1,0:T(8,128)(2,1)S(1)} %get-tuple-element.36), channel_id=1, source_target_pairs={{0,16},{16,32},{32,48},{48,64},{64,80},{80,96},{96,112},{112,128},... | collective-permute-start | bytes 147464 | tf_op jit(solution)/shard_map/ppermute | solution.py:20
  15.3 1.9 collective-permute-start.1
  20.5 1.2 reduce.5
  25.2 1.1 copy-done
  26.4 10.5 %forward.1 = (bf16[256,2304]{1,0:T(8,128)(2,1)S(1)}, bf16[256,2304]{1,0:T(8,128)(2,1)S(1)}, bf16[256,768]{1,0:T(8,128)(2,1)S(1)}, bf16[256,1536]{1,0:T(8,128)(2,1)}, f32[256,768]{1,0:T(8,128)}) custom-call(s32[2]{0:T(128)S(1)} %pad_add_fusion.base_ref, bf16[32,1536]{1,0:T(8,128)(2,1)S(1)} %pad_maximum_fusion.14.edge_ref, bf16[256,1536]{1,0:T(8,128)(2,1)S(1)} %bitcast.112, ...), custom_call_target="tpu_custom_call" | custom-call | flops 3019898880 | bytes 12582912 | tf_op jit(solution)/shard_map/forward/pallas_call | solution.py:241
  36.8 1.1 copy-done.2
  40.8 1.4 select_reduce_fusion
  42.2 1.0 fusion.67
  43.8 1.3 fusion.85
  45.1 1.3 eq.79
  49.6 1.9 collective-permute-start.3
  51.5 1.5 collective-permute-start.5
  53.0 1.6 collective-permute-start.4
  54.6 5.1 %collective-permute-done.3 = bf16[64,2304]{1,0:T(8,128)(2,1)S(1)} collective-permute-done((bf16[64,2304]{1,0:T(8,128)(2,1)S(1)}, bf16[64,2304]{1,0:T(8,128)(2,1)S(1)}, u32[]{:S(2)}, u32[]{:S(2)}) %collective-permute-start.3) | collective-permute-done | bytes 294944 | tf_op jit(solution)/shard_map/ppermute | solution.py:15
  60.4 14.3 %collective-permute-start.21 = (bf16[288,1536]{1,0:T(8,128)(2,1)S(1)}, bf16[288,1536]{1,0:T(8,128)(2,1)S(1)}, u32[]{:S(2)}, u32[]{:S(2)}) collective-permute-start(bf16[288,1536]{1,0:T(8,128)(2,1)S(1)} %pad_maximum_fusion.1), channel_id=1, source_target_pairs={{0,240},{16,224},{32,208},{48,192},{64,176},{80,160},{96,144},{112... | collective-permute-start | bytes 2654216 | tf_op jit(solution)/shard_map/ppermute | solution.py:354
  75.2 29.4 %collective-permute-done.21.padded_ref = bf16[288,1536]{1,0:T(8,128)(2,1)S(1)} collective-permute-done((bf16[288,1536]{1,0:T(8,128)(2,1)S(1)}, bf16[288,1536]{1,0:T(8,128)(2,1)S(1)}, u32[]{:S(2)}, u32[]{:S(2)}) %collective-permute-start.21) | collective-permute-done | bytes 884768 | tf_op jit(solution)/shard_map/ppermute | solution.py:354
  104.6 11.1 %reflect.1 = (f32[256,1536]{1,0:T(8,128)S(1)}, bf16[256,1536]{1,0:T(8,128)(2,1)S(1)}) custom-call(bf16[288,1536]{1,0:T(8,128)(2,1)S(1)} %collective-permute-done.21.padded_ref, f32[1,1536]{1,0:T(1,128)S(1)} %broadcast_in_dim.77.gain_ref, bf16[256,1536]{1,0:T(8,128)(2,1)S(1)} %copy-done.3, s32[1,1536]{1,0:T(1,128)S(1)} %broadcast_in_dim.86.perm_ref, ...), custom_call_target="tpu_custom_call" | custom-call | flops 4831838208 | bytes 13369344 | tf_op jit(solution)/shard_map/reflect/pallas_call | solution.py:191
  115.9 8.1 %collective-permute-start.7 = (bf16[36,2304]{1,0:T(8,128)(2,1)S(1)}, bf16[36,2304]{1,0:T(8,128)(2,1)S(1)}, u32[]{:S(2)}, u32[]{:S(2)}) collective-permute-start(bf16[36,2304]{1,0:T(8,128)(2,1)S(1)} %get-tuple-element.50), channel_id=1, source_target_pairs={{0,1},{1,2},{2,3},{3,0},{4,5},{5,6},{6,7},{7,4},{8,9},{9,10},{10,1... | collective-permute-start | bytes 497672 | tf_op jit(solution)/shard_map/ppermute | solution.py:15
  124.0 6.0 %collective-permute-start.8 = (bf16[36,2304]{1,0:T(8,128)(2,1)S(1)}, bf16[36,2304]{1,0:T(8,128)(2,1)S(1)}, u32[]{:S(2)}, u32[]{:S(2)}) collective-permute-start(bf16[36,2304]{1,0:T(8,128)(2,1)S(1)} %get-tuple-element.51), channel_id=1, source_target_pairs={{0,2},{1,3},{2,0},{3,1},{4,6},{5,7},{6,4},{7,5},{8,10},{9,11},{10,... | collective-permute-start | bytes 497672 | tf_op jit(solution)/shard_map/ppermute | solution.py:15
  130.1 4.0 %collective-permute-done.7 = bf16[36,2304]{1,0:T(8,128)(2,1)S(1)} collective-permute-done((bf16[36,2304]{1,0:T(8,128)(2,1)S(1)}, bf16[36,2304]{1,0:T(8,128)(2,1)S(1)}, u32[]{:S(2)}, u32[]{:S(2)}) %collective-permute-start.7) | collective-permute-done | bytes 165920 | tf_op jit(solution)/shard_map/ppermute | solution.py:15
  134.1 1.1 collective-permute-start.9
  135.5 7.2 %collective-permute-done.8 = bf16[36,2304]{1,0:T(8,128)(2,1)S(1)} collective-permute-done((bf16[36,2304]{1,0:T(8,128)(2,1)S(1)}, bf16[36,2304]{1,0:T(8,128)(2,1)S(1)}, u32[]{:S(2)}, u32[]{:S(2)}) %collective-permute-start.8) | collective-permute-done | bytes 165920 | tf_op jit(solution)/shard_map/ppermute | solution.py:15
  142.7 1.8 collective-permute-done.9
  144.8 2.4 %fusion.38 = (f32[16,1024]{1,0:T(8,128)S(1)}, f32[128,1024]{1,0:T(8,128)S(1)}) fusion(pred[16,8]{1,0:T(8,128)(4,1)S(1)} %iota_compare_fusion, bf16[256,1536]{0,1:T(8,128)(2,1)} %collective-permute-done.12, bf16[256,1536]{0,1:T(8,128)(2,1)} %collective-permute-done.11, bf16[256,1536]{0,1:T(8,128)(2,1)S(1)} %collective-permute-done.10, ...), kind=kOutput, calls=%fused_computation.58 | convolution fusion | flops 418103296 | bytes 4128896 | tf_op jit(solution)/shard_map/dot_general | solution.py:45
  147.2 2.6 %convolution_convert_fusion = bf16[128,1536]{1,0:T(8,128)(2,1)S(1)} fusion(bf16[256,1536]{0,1:T(8,128)(2,1)} %collective-permute-done.12, bf16[256,1536]{0,1:T(8,128)(2,1)} %collective-permute-done.11, bf16[256,1536]{0,1:T(8,128)(2,1)S(1)} %collective-permute-done.10, bf16[256,1536]{0,1:T(8,128)(2,1)S(1)} %bitcast.136, ...), kind=kOutput, calls=%fused_computation.12 | convolution fusion | flops 416088064 | bytes 4128768 | tf_op jit(solution)/shard_map/dot_general | solution.py:45
  149.9 4.1 %collective-permute-start.13 = (bf16[32,1536]{1,0:T(8,128)(2,1)S(1)}, bf16[32,1536]{1,0:T(8,128)(2,1)S(1)}, u32[]{:S(2)}, u32[]{:S(2)}) collective-permute-start(bf16[32,1536]{1,0:T(8,128)(2,1)S(1)} %get-tuple-element.42), channel_id=1, source_target_pairs={{0,3},{1,0},{2,1},{3,2},{4,7},{5,4},{6,5},{7,6},{8,11},{9,8},{10,9... | collective-permute-start | bytes 294920 | tf_op jit(solution)/shard_map/ppermute | solution.py:15
  155.6 3.7 %collective-permute-done.15 = bf16[32,1536]{1,0:T(8,128)(2,1)S(1)} collective-permute-done((bf16[32,1536]{1,0:T(8,128)(2,1)S(1)}, bf16[32,1536]{1,0:T(8,128)(2,1)S(1)}, u32[]{:S(2)}, u32[]{:S(2)}) %collective-permute-start.15) | collective-permute-done | bytes 98336 | tf_op jit(solution)/shard_map/ppermute | solution.py:15
  159.3 1.2 collective-permute-done.14
  161.8 5.6 %collective-permute-start.24 = (bf16[768,768]{1,0:T(8,128)(2,1)S(1)}, bf16[768,768]{1,0:T(8,128)(2,1)S(1)}, u32[]{:S(2)}, u32[]{:S(2)}) collective-permute-start(bf16[768,768]{1,0:T(8,128)(2,1)S(1)} %add_convert_fusion.1), channel_id=1, source_target_pairs={{0,16},{16,0},{1,17},{17,1},{2,18},{18,2},{3,19},{19,3},{4,20},{20... | collective-permute-start | bytes 3538952 | tf_op jit(solution)/shard_map/ppermute | solution.py:15
  168.9 2.5 %collective-permute-start.17 = (bf16[64,1536]{1,0:T(8,128)(2,1)S(1)}, bf16[64,1536]{1,0:T(8,128)(2,1)S(1)}, u32[]{:S(2)}, u32[]{:S(2)}) collective-permute-start(bf16[64,1536]{1,0:T(8,128)(2,1)S(1)} %pad_maximum_fusion.9), channel_id=1, source_target_pairs={{0,192},{64,0},{128,64},{192,128},{1,193},{65,1},{129,65},{193,129... | collective-permute-start | bytes 589832 | tf_op jit(solution)/shard_map/ppermute | solution.py:15
  171.4 5.5 %collective-permute-done.17 = bf16[64,1536]{1,0:T(8,128)(2,1)S(1)} collective-permute-done((bf16[64,1536]{1,0:T(8,128)(2,1)S(1)}, bf16[64,1536]{1,0:T(8,128)(2,1)S(1)}, u32[]{:S(2)}, u32[]{:S(2)}) %collective-permute-start.17) | collective-permute-done | bytes 196640 | tf_op jit(solution)/shard_map/ppermute | solution.py:15
  176.9 7.2 %collective-permute-start.20 = (bf16[256,1536]{1,0:T(8,128)(2,1)S(1)}, bf16[256,1536]{1,0:T(8,128)(2,1)S(1)}, u32[]{:S(2)}, u32[]{:S(2)}) collective-permute-start(bf16[256,1536]{1,0:T(8,128)(2,1)S(1)} %constant_dynamic-update-slice_fusion), channel_id=1, source_target_pairs={{0,16},{16,0},{1,17},{17,1},{2,18},{18,2},{3,19},{19,3},{4,20},{20... | collective-permute-start | bytes 2359304 | tf_op jit(solution)/shard_map/ppermute | solution.py:15
  186.2 2.1 collective-permute-start.27
  188.3 1.2 collective-permute-start.26
  192.1 2.9 %collective-permute-start.22 = (bf16[16,768]{1,0:T(8,128)(2,1)S(1)}, bf16[16,768]{1,0:T(8,128)(2,1)S(1)}, u32[]{:S(2)}, u32[]{:S(2)}) collective-permute-start(bf16[16,768]{1,0:T(8,128)(2,1)S(1)} %get-tuple-element.40), channel_id=1, source_target_pairs={{16,0},{32,16},{48,32},{64,48},{80,64},{96,80},{112,96},{128,112},... | collective-permute-start | bytes 73736 | tf_op jit(solution)/shard_map/ppermute | solution.py:21
  195.0 6.7 %collective-permute-start.23 = (bf16[16,768]{1,0:T(8,128)(2,1)S(1)}, bf16[16,768]{1,0:T(8,128)(2,1)S(1)}, u32[]{:S(2)}, u32[]{:S(2)}) collective-permute-start(bf16[16,768]{1,0:T(8,128)(2,1)S(1)} %get-tuple-element.41), channel_id=1, source_target_pairs={{0,16},{16,32},{32,48},{48,64},{64,80},{80,96},{96,112},{112,128},... | collective-permute-start | bytes 73736 | tf_op jit(solution)/shard_map/ppermute | solution.py:20
  202.8 1.1 collective-permute-start.28
  203.9 2.4 %collective-permute-start.30 = (bf16[48,768]{1,0:T(8,128)(2,1)S(1)}, bf16[48,768]{1,0:T(8,128)(2,1)S(1)}, u32[]{:S(2)}, u32[]{:S(2)}) collective-permute-start(bf16[48,768]{1,0:T(8,128)(2,1)S(1)} %get-tuple-element.48), channel_id=1, source_target_pairs={{0,3},{1,0},{2,1},{3,2},{4,7},{5,4},{6,5},{7,6},{8,11},{9,8},{10,9... | collective-permute-start | bytes 221192 | tf_op jit(solution)/shard_map/ppermute | solution.py:15
  207.3 1.4 collective-permute-done.28
  208.7 5.1 %collective-permute-done.29 = bf16[48,768]{1,0:T(8,128)(2,1)S(1)} collective-permute-done((bf16[48,768]{1,0:T(8,128)(2,1)S(1)}, bf16[48,768]{1,0:T(8,128)(2,1)S(1)}, u32[]{:S(2)}, u32[]{:S(2)}) %collective-permute-start.29) | collective-permute-done | bytes 73760 | tf_op jit(solution)/shard_map/ppermute | solution.py:15
  213.8 2.1 collective-permute-start.33
  215.9 1.3 collective-permute-start.31
  217.1 1.6 fusion.27
  218.7 3.8 %collective-permute-done.32 = bf16[48,768]{1,0:T(8,128)(2,1)S(1)} collective-permute-done((bf16[48,768]{1,0:T(8,128)(2,1)S(1)}, bf16[48,768]{1,0:T(8,128)(2,1)S(1)}, u32[]{:S(2)}, u32[]{:S(2)}) %collective-permute-start.32) | collective-permute-done | bytes 73760 | tf_op jit(solution)/shard_map/ppermute | solution.py:15
  222.7 7.1 %collective-permute-done.34 = bf16[48,768]{1,0:T(8,128)(2,1)S(1)} collective-permute-done((bf16[48,768]{1,0:T(8,128)(2,1)S(1)}, bf16[48,768]{1,0:T(8,128)(2,1)S(1)}, u32[]{:S(2)}, u32[]{:S(2)}) %collective-permute-start.34) | collective-permute-done | bytes 73760 | tf_op jit(solution)/shard_map/ppermute | solution.py:15
  229.8 2.0 collective-permute-start.35
  231.8 1.3 fusion.33
  (152 shorter events, 28.3 us)
Async XLA Ops:
  0.6 144.1 %collective-permute-start.12 = (bf16[256,1536]{0,1:T(8,128)(2,1)}, bf16[256,1536]{0,1:T(8,128)(2,1)}, u32[]{:S(2)}, u32[]{:S(2)}) collective-permute-start(bf16[256,1536]{0,1:T(8,128)(2,1)} %bitcast.132), channel_id=1, source_target_pairs={{0,12},{4,0},{8,4},{12,8},{1,13},{5,1},{9,5},{13,9},{2,14},{6,2},{... | collective-permute-start | bytes 2359304 | tf_op jit(solution)/shard_map/ppermute | solution.py:15
  4.0 140.8 %collective-permute-start.11 = (bf16[256,1536]{0,1:T(8,128)(2,1)}, bf16[256,1536]{0,1:T(8,128)(2,1)}, u32[]{:S(2)}, u32[]{:S(2)}) collective-permute-start(bf16[256,1536]{0,1:T(8,128)(2,1)} %bitcast.133), channel_id=1, source_target_pairs={{0,8},{4,12},{8,0},{12,4},{1,9},{5,13},{9,1},{13,5},{2,10},{6,14},... | collective-permute-start | bytes 2359304 | tf_op jit(solution)/shard_map/ppermute | solution.py:15
  5.4 19.1 %collective-permute-start = (bf16[16,1536]{1,0:T(8,128)(2,1)S(1)}, bf16[16,1536]{1,0:T(8,128)(2,1)S(1)}, u32[]{:S(2)}, u32[]{:S(2)}) collective-permute-start(bf16[16,1536]{1,0:T(8,128)(2,1)S(1)} %get-tuple-element.36), channel_id=1, source_target_pairs={{0,16},{16,32},{32,48},{48,64},{64,80},{80,96},{96,112},{112,128},... | collective-permute-start | bytes 147464 | tf_op jit(solution)/shard_map/ppermute | solution.py:20
  15.3 9.3 %collective-permute-start.1 = (bf16[16,1536]{1,0:T(8,128)(2,1)S(1)}, bf16[16,1536]{1,0:T(8,128)(2,1)S(1)}, u32[]{:S(2)}, u32[]{:S(2)}) collective-permute-start(bf16[16,1536]{1,0:T(8,128)(2,1)S(1)} %get-tuple-element.37), channel_id=1, source_target_pairs={{16,0},{32,16},{48,32},{64,48},{80,64},{96,80},{112,96},{128,112},... | collective-permute-start | bytes 147464 | tf_op jit(solution)/shard_map/ppermute | solution.py:21
  25.2 1.1 copy-start
  26.4 11.5 %copy-start.4 = (f32[1,4,4096]{2,1,0:T(4,128)S(1)}, f32[1,4,4096]{2,1,0:T(4,128)}, u32[]{:S(2)}) copy-start(f32[1,4,4096]{2,1,0:T(4,128)} %param.19) | copy-start | bytes 196612
  26.4 20.9 %copy-start.1 = (bf16[1,256,1536]{2,1,0:T(8,128)(2,1)S(1)}, bf16[1,256,1536]{2,1,0:T(8,128)(2,1)}, u32[]{:S(2)}) copy-start(bf16[1,256,1536]{2,1,0:T(8,128)(2,1)} %param.10) | copy-start | bytes 2359300
  40.0 9.1 %collective-permute-start.2 = (bf16[256,2304]{1,0:T(8,128)(2,1)}, bf16[256,2304]{1,0:T(8,128)(2,1)S(1)}, u32[]{:S(2)}, u32[]{:S(2)}) collective-permute-start(bf16[256,2304]{1,0:T(8,128)(2,1)} %copy-done.2), channel_id=1, source_target_pairs={{0,16},{16,0},{1,17},{17,1},{2,18},{18,2},{3,19},{19,3},{4,20},{20... | collective-permute-start | bytes 3538952 | tf_op jit(solution)/shard_map/ppermute | solution.py:15
  49.5 5.1 %copy-start.6 = (bf16[16,1536]{1,0:T(8,128)(2,1)S(1)}, bf16[16,1536]{1,0:T(8,128)(2,1)}, u32[]{:S(2)}) copy-start(bf16[16,1536]{1,0:T(8,128)(2,1)} %copy-done.5) | copy-start | bytes 147460
  49.5 5.1 %copy-start.8 = (bf16[16,1536]{1,0:T(8,128)(2,1)S(1)}, bf16[16,1536]{1,0:T(8,128)(2,1)}, u32[]{:S(2)}) copy-start(bf16[16,1536]{1,0:T(8,128)(2,1)} %copy-done.7) | copy-start | bytes 147460
  49.5 10.3 %copy-start.11 = (bf16[1536,256]{1,0:T(8,128)(2,1)S(1)}, bf16[1536,256]{1,0:T(8,128)(2,1)}, u32[]{:S(2)}) copy-start(bf16[1536,256]{1,0:T(8,128)(2,1)} %param.14) | copy-start | bytes 2359300
  49.6 10.2 %collective-permute-start.3 = (bf16[64,2304]{1,0:T(8,128)(2,1)S(1)}, bf16[64,2304]{1,0:T(8,128)(2,1)S(1)}, u32[]{:S(2)}, u32[]{:S(2)}) collective-permute-start(bf16[64,2304]{1,0:T(8,128)(2,1)S(1)} %get-tuple-element.31), channel_id=1, source_target_pairs={{0,64},{64,128},{128,192},{192,0},{1,65},{65,129},{129,193},{193,1... | collective-permute-start | bytes 884744 | tf_op jit(solution)/shard_map/ppermute | solution.py:15
  51.5 8.9 %collective-permute-start.5 = (bf16[64,2304]{1,0:T(8,128)(2,1)S(1)}, bf16[64,2304]{1,0:T(8,128)(2,1)S(1)}, u32[]{:S(2)}, u32[]{:S(2)}) collective-permute-start(bf16[64,2304]{1,0:T(8,128)(2,1)S(1)} %get-tuple-element.32), channel_id=1, source_target_pairs={{0,192},{64,0},{128,64},{192,128},{1,193},{65,1},{129,65},{193,129... | collective-permute-start | bytes 884744 | tf_op jit(solution)/shard_map/ppermute | solution.py:15
  53.0 21.7 %collective-permute-start.4 = (bf16[64,2304]{1,0:T(8,128)(2,1)S(1)}, bf16[64,2304]{1,0:T(8,128)(2,1)S(1)}, u32[]{:S(2)}, u32[]{:S(2)}) collective-permute-start(bf16[64,2304]{1,0:T(8,128)(2,1)S(1)} %get-tuple-element.33), channel_id=1, source_target_pairs={{0,128},{64,192},{128,0},{192,64},{1,129},{65,193},{129,1},{193,65... | collective-permute-start | bytes 884744 | tf_op jit(solution)/shard_map/ppermute | solution.py:15
  54.6 50.1 %copy-start.3 = (bf16[256,1536]{1,0:T(8,128)(2,1)S(1)}, bf16[256,1536]{1,0:T(8,128)(2,1)}, u32[]{:S(2)}) copy-start(bf16[256,1536]{1,0:T(8,128)(2,1)} %get-tuple-element.14.own_ref) | copy-start | bytes 2359300
  59.8 85.0 %collective-permute-start.10 = (bf16[256,1536]{0,1:T(8,128)(2,1)S(1)}, bf16[256,1536]{0,1:T(8,128)(2,1)S(1)}, u32[]{:S(2)}, u32[]{:S(2)}) collective-permute-start(bf16[256,1536]{0,1:T(8,128)(2,1)S(1)} %bitcast.134), channel_id=1, source_target_pairs={{0,4},{4,8},{8,12},{12,0},{1,5},{5,9},{9,13},{13,1},{2,6},{6,10},{... | collective-permute-start | bytes 2359304 | tf_op jit(solution)/shard_map/ppermute | solution.py:15
  60.4 44.2 %collective-permute-start.21 = (bf16[288,1536]{1,0:T(8,128)(2,1)S(1)}, bf16[288,1536]{1,0:T(8,128)(2,1)S(1)}, u32[]{:S(2)}, u32[]{:S(2)}) collective-permute-start(bf16[288,1536]{1,0:T(8,128)(2,1)S(1)} %pad_maximum_fusion.1), channel_id=1, source_target_pairs={{0,240},{16,224},{32,208},{48,192},{64,176},{80,160},{96,144},{112... | collective-permute-start | bytes 2654216 | tf_op jit(solution)/shard_map/ppermute | solution.py:354
  74.9 40.9 %collective-permute-start.6 = (bf16[32,2304]{1,0:T(8,128)(2,1)S(1)}, bf16[32,2304]{1,0:T(8,128)(2,1)S(1)}, u32[]{:S(2)}, u32[]{:S(2)}) collective-permute-start(bf16[32,2304]{1,0:T(8,128)(2,1)S(1)} %dynamic-slice_bitcast_fusion.6), channel_id=1, source_target_pairs={{0,32},{32,0},{1,33},{33,1},{2,34},{34,2},{3,35},{35,3},{4,36},{36... | collective-permute-start | bytes 442376 | tf_op jit(solution)/shard_map/ppermute | solution.py:15
  115.9 18.2 %collective-permute-start.7 = (bf16[36,2304]{1,0:T(8,128)(2,1)S(1)}, bf16[36,2304]{1,0:T(8,128)(2,1)S(1)}, u32[]{:S(2)}, u32[]{:S(2)}) collective-permute-start(bf16[36,2304]{1,0:T(8,128)(2,1)S(1)} %get-tuple-element.50), channel_id=1, source_target_pairs={{0,1},{1,2},{2,3},{3,0},{4,5},{5,6},{6,7},{7,4},{8,9},{9,10},{10,1... | collective-permute-start | bytes 497672 | tf_op jit(solution)/shard_map/ppermute | solution.py:15
  124.0 18.6 %collective-permute-start.8 = (bf16[36,2304]{1,0:T(8,128)(2,1)S(1)}, bf16[36,2304]{1,0:T(8,128)(2,1)S(1)}, u32[]{:S(2)}, u32[]{:S(2)}) collective-permute-start(bf16[36,2304]{1,0:T(8,128)(2,1)S(1)} %get-tuple-element.51), channel_id=1, source_target_pairs={{0,2},{1,3},{2,0},{3,1},{4,6},{5,7},{6,4},{7,5},{8,10},{9,11},{10,... | collective-permute-start | bytes 497672 | tf_op jit(solution)/shard_map/ppermute | solution.py:15
  134.1 10.3 %collective-permute-start.9 = (bf16[36,2304]{1,0:T(8,128)(2,1)S(1)}, bf16[36,2304]{1,0:T(8,128)(2,1)S(1)}, u32[]{:S(2)}, u32[]{:S(2)}) collective-permute-start(bf16[36,2304]{1,0:T(8,128)(2,1)S(1)} %get-tuple-element.52), channel_id=1, source_target_pairs={{0,3},{1,0},{2,1},{3,2},{4,7},{5,4},{6,5},{7,6},{8,11},{9,8},{10,9... | collective-permute-start | bytes 497672 | tf_op jit(solution)/shard_map/ppermute | solution.py:15
  149.9 5.7 %collective-permute-start.13 = (bf16[32,1536]{1,0:T(8,128)(2,1)S(1)}, bf16[32,1536]{1,0:T(8,128)(2,1)S(1)}, u32[]{:S(2)}, u32[]{:S(2)}) collective-permute-start(bf16[32,1536]{1,0:T(8,128)(2,1)S(1)} %get-tuple-element.42), channel_id=1, source_target_pairs={{0,3},{1,0},{2,1},{3,2},{4,7},{5,4},{6,5},{7,6},{8,11},{9,8},{10,9... | collective-permute-start | bytes 294920 | tf_op jit(solution)/shard_map/ppermute | solution.py:15
  154.0 5.4 %collective-permute-start.15 = (bf16[32,1536]{1,0:T(8,128)(2,1)S(1)}, bf16[32,1536]{1,0:T(8,128)(2,1)S(1)}, u32[]{:S(2)}, u32[]{:S(2)}) collective-permute-start(bf16[32,1536]{1,0:T(8,128)(2,1)S(1)} %get-tuple-element.43), channel_id=1, source_target_pairs={{0,1},{1,2},{2,3},{3,0},{4,5},{5,6},{6,7},{7,4},{8,9},{9,10},{10,1... | collective-permute-start | bytes 294920 | tf_op jit(solution)/shard_map/ppermute | solution.py:15
  154.0 6.5 %collective-permute-start.14 = (bf16[32,1536]{1,0:T(8,128)(2,1)S(1)}, bf16[32,1536]{1,0:T(8,128)(2,1)S(1)}, u32[]{:S(2)}, u32[]{:S(2)}) collective-permute-start(bf16[32,1536]{1,0:T(8,128)(2,1)S(1)} %get-tuple-element.44), channel_id=1, source_target_pairs={{0,2},{1,3},{2,0},{3,1},{4,6},{5,7},{6,4},{7,5},{8,10},{9,11},{10,... | collective-permute-start | bytes 294920 | tf_op jit(solution)/shard_map/ppermute | solution.py:15
  160.6 7.8 %collective-permute-start.16 = (bf16[32,1536]{1,0:T(8,128)(2,1)S(1)}, bf16[32,1536]{1,0:T(8,128)(2,1)S(1)}, u32[]{:S(2)}, u32[]{:S(2)}) collective-permute-start(bf16[32,1536]{1,0:T(8,128)(2,1)S(1)} %get-tuple-element.27), channel_id=1, source_target_pairs={{0,32},{32,0},{1,33},{33,1},{2,34},{34,2},{3,35},{35,3},{4,36},{36... | collective-permute-start | bytes 294920 | tf_op jit(solution)/shard_map/ppermute | solution.py:15
  161.8 22.8 %collective-permute-start.24 = (bf16[768,768]{1,0:T(8,128)(2,1)S(1)}, bf16[768,768]{1,0:T(8,128)(2,1)S(1)}, u32[]{:S(2)}, u32[]{:S(2)}) collective-permute-start(bf16[768,768]{1,0:T(8,128)(2,1)S(1)} %add_convert_fusion.1), channel_id=1, source_target_pairs={{0,16},{16,0},{1,17},{17,1},{2,18},{18,2},{3,19},{19,3},{4,20},{20... | collective-permute-start | bytes 3538952 | tf_op jit(solution)/shard_map/ppermute | solution.py:15
  168.3 8.6 %collective-permute-start.19 = (bf16[64,1536]{1,0:T(8,128)(2,1)S(1)}, bf16[64,1536]{1,0:T(8,128)(2,1)S(1)}, u32[]{:S(2)}, u32[]{:S(2)}) collective-permute-start(bf16[64,1536]{1,0:T(8,128)(2,1)S(1)} %pad_maximum_fusion.9), channel_id=1, source_target_pairs={{0,64},{64,128},{128,192},{192,0},{1,65},{65,129},{129,193},{193,1... | collective-permute-start | bytes 589832 | tf_op jit(solution)/shard_map/ppermute | solution.py:15
  168.9 8.0 %collective-permute-start.18 = (bf16[64,1536]{1,0:T(8,128)(2,1)S(1)}, bf16[64,1536]{1,0:T(8,128)(2,1)S(1)}, u32[]{:S(2)}, u32[]{:S(2)}) collective-permute-start(bf16[64,1536]{1,0:T(8,128)(2,1)S(1)} %pad_maximum_fusion.9), channel_id=1, source_target_pairs={{0,128},{64,192},{128,0},{192,64},{1,129},{65,193},{129,1},{193,65... | collective-permute-start | bytes 589832 | tf_op jit(solution)/shard_map/ppermute | solution.py:15
  168.9 8.0 %collective-permute-start.17 = (bf16[64,1536]{1,0:T(8,128)(2,1)S(1)}, bf16[64,1536]{1,0:T(8,128)(2,1)S(1)}, u32[]{:S(2)}, u32[]{:S(2)}) collective-permute-start(bf16[64,1536]{1,0:T(8,128)(2,1)S(1)} %pad_maximum_fusion.9), channel_id=1, source_target_pairs={{0,192},{64,0},{128,64},{192,128},{1,193},{65,1},{129,65},{193,129... | collective-permute-start | bytes 589832 | tf_op jit(solution)/shard_map/ppermute | solution.py:15
  176.9 12.6 %collective-permute-start.20 = (bf16[256,1536]{1,0:T(8,128)(2,1)S(1)}, bf16[256,1536]{1,0:T(8,128)(2,1)S(1)}, u32[]{:S(2)}, u32[]{:S(2)}) collective-permute-start(bf16[256,1536]{1,0:T(8,128)(2,1)S(1)} %constant_dynamic-update-slice_fusion), channel_id=1, source_target_pairs={{0,16},{16,0},{1,17},{17,1},{2,18},{18,2},{3,19},{19,3},{4,20},{20... | collective-permute-start | bytes 2359304 | tf_op jit(solution)/shard_map/ppermute | solution.py:15
  185.2 5.1 %copy-start.12 = (f32[256,768]{1,0:T(8,128)S(1)}, f32[256,768]{1,0:T(8,128)}, u32[]{:S(2)}) copy-start(f32[256,768]{1,0:T(8,128)} %get-tuple-element.23) | copy-start | bytes 2359300
  185.3 17.3 %collective-permute-start.25 = (bf16[192,768]{1,0:T(8,128)(2,1)S(1)}, bf16[192,768]{1,0:T(8,128)(2,1)S(1)}, u32[]{:S(2)}, u32[]{:S(2)}) collective-permute-start(bf16[192,768]{1,0:T(8,128)(2,1)S(1)} %get-tuple-element.28), channel_id=1, source_target_pairs={{0,4},{4,8},{8,12},{12,0},{1,5},{5,9},{9,13},{13,1},{2,6},{6,10},{... | collective-permute-start | bytes 884744 | tf_op jit(solution)/shard_map/ppermute | solution.py:15
  186.2 16.4 %collective-permute-start.27 = (bf16[192,768]{1,0:T(8,128)(2,1)S(1)}, bf16[192,768]{1,0:T(8,128)(2,1)S(1)}, u32[]{:S(2)}, u32[]{:S(2)}) collective-permute-start(bf16[192,768]{1,0:T(8,128)(2,1)S(1)} %get-tuple-element.29), channel_id=1, source_target_pairs={{0,12},{4,0},{8,4},{12,8},{1,13},{5,1},{9,5},{13,9},{2,14},{6,2},{... | collective-permute-start | bytes 884744 | tf_op jit(solution)/shard_map/ppermute | solution.py:15
  188.3 14.3 %collective-permute-start.26 = (bf16[192,768]{1,0:T(8,128)(2,1)S(1)}, bf16[192,768]{1,0:T(8,128)(2,1)S(1)}, u32[]{:S(2)}, u32[]{:S(2)}) collective-permute-start(bf16[192,768]{1,0:T(8,128)(2,1)S(1)} %get-tuple-element.30), channel_id=1, source_target_pairs={{0,8},{4,12},{8,0},{12,4},{1,9},{5,13},{9,1},{13,5},{2,10},{6,14},... | collective-permute-start | bytes 884744 | tf_op jit(solution)/shard_map/ppermute | solution.py:15
  189.5 1.7 copy-start.10
  189.5 12.2 %slice-start = ((s8[7077888]{0:T(1024)(128)(4,1)}), s8[4194304]{0:T(1024)(128)(4,1)S(1)}, s32[]{:S(2)}) async-start(s8[7077888]{0:T(1024)(128)(4,1)} %bitcast.130), calls=%async_computation | async-start | bytes 8388608
  189.9 11.8 %slice-start.1 = ((s8[7077888]{0:T(1024)(128)(4,1)}), s8[2883584]{0:T(1024)(128)(4,1)S(1)}, s32[]{:S(2)}) async-start(s8[7077888]{0:T(1024)(128)(4,1)} %bitcast.130), calls=%async_computation.1 | async-start | bytes 5767168
  192.1 25.0 %collective-permute-start.22 = (bf16[16,768]{1,0:T(8,128)(2,1)S(1)}, bf16[16,768]{1,0:T(8,128)(2,1)S(1)}, u32[]{:S(2)}, u32[]{:S(2)}) collective-permute-start(bf16[16,768]{1,0:T(8,128)(2,1)S(1)} %get-tuple-element.40), channel_id=1, source_target_pairs={{16,0},{32,16},{48,32},{64,48},{80,64},{96,80},{112,96},{128,112},... | collective-permute-start | bytes 73736 | tf_op jit(solution)/shard_map/ppermute | solution.py:21
  195.0 11.5 %collective-permute-start.23 = (bf16[16,768]{1,0:T(8,128)(2,1)S(1)}, bf16[16,768]{1,0:T(8,128)(2,1)S(1)}, u32[]{:S(2)}, u32[]{:S(2)}) collective-permute-start(bf16[16,768]{1,0:T(8,128)(2,1)S(1)} %get-tuple-element.41), channel_id=1, source_target_pairs={{0,16},{16,32},{32,48},{48,64},{64,80},{80,96},{96,112},{112,128},... | collective-permute-start | bytes 73736 | tf_op jit(solution)/shard_map/ppermute | solution.py:20
  202.8 5.9 %collective-permute-start.28 = (bf16[48,768]{1,0:T(8,128)(2,1)S(1)}, bf16[48,768]{1,0:T(8,128)(2,1)S(1)}, u32[]{:S(2)}, u32[]{:S(2)}) collective-permute-start(bf16[48,768]{1,0:T(8,128)(2,1)S(1)} %get-tuple-element.47), channel_id=1, source_target_pairs={{0,1},{1,2},{2,3},{3,0},{4,5},{5,6},{6,7},{7,4},{8,9},{9,10},{10,1... | collective-permute-start | bytes 221192 | tf_op jit(solution)/shard_map/ppermute | solution.py:15
  203.9 4.8 %collective-permute-start.30 = (bf16[48,768]{1,0:T(8,128)(2,1)S(1)}, bf16[48,768]{1,0:T(8,128)(2,1)S(1)}, u32[]{:S(2)}, u32[]{:S(2)}) collective-permute-start(bf16[48,768]{1,0:T(8,128)(2,1)S(1)} %get-tuple-element.48), channel_id=1, source_target_pairs={{0,3},{1,0},{2,1},{3,2},{4,7},{5,4},{6,5},{7,6},{8,11},{9,8},{10,9... | collective-permute-start | bytes 221192 | tf_op jit(solution)/shard_map/ppermute | solution.py:15
  206.3 10.9 %copy-start.9 = (f32[1536]{0:T(1024)S(1)}, f32[1536]{0:T(1024)}, u32[]{:S(2)}) copy-start(f32[1536]{0:T(1024)} %param.11) | copy-start | bytes 18436
  206.3 7.4 %collective-permute-start.29 = (bf16[48,768]{1,0:T(8,128)(2,1)S(1)}, bf16[48,768]{1,0:T(8,128)(2,1)S(1)}, u32[]{:S(2)}, u32[]{:S(2)}) collective-permute-start(bf16[48,768]{1,0:T(8,128)(2,1)S(1)} %get-tuple-element.49), channel_id=1, source_target_pairs={{0,2},{1,3},{2,0},{3,1},{4,6},{5,7},{6,4},{7,5},{8,10},{9,11},{10,... | collective-permute-start | bytes 221192 | tf_op jit(solution)/shard_map/ppermute | solution.py:15
  213.8 4.9 %collective-permute-start.33 = (bf16[48,768]{1,0:T(8,128)(2,1)S(1)}, bf16[48,768]{1,0:T(8,128)(2,1)S(1)}, u32[]{:S(2)}, u32[]{:S(2)}) collective-permute-start(bf16[48,768]{1,0:T(8,128)(2,1)S(1)} %fusion.63), channel_id=1, source_target_pairs={{0,192},{64,0},{128,64},{192,128},{1,193},{65,1},{129,65},{193,129... | collective-permute-start | bytes 221192 | tf_op jit(solution)/shard_map/ppermute | solution.py:15
  215.9 6.7 %collective-permute-start.32 = (bf16[48,768]{1,0:T(8,128)(2,1)S(1)}, bf16[48,768]{1,0:T(8,128)(2,1)S(1)}, u32[]{:S(2)}, u32[]{:S(2)}) collective-permute-start(bf16[48,768]{1,0:T(8,128)(2,1)S(1)} %fusion.63), channel_id=1, source_target_pairs={{0,64},{64,128},{128,192},{192,0},{1,65},{65,129},{129,193},{193,1... | collective-permute-start | bytes 221192 | tf_op jit(solution)/shard_map/ppermute | solution.py:15
  215.9 6.7 %collective-permute-start.31 = (bf16[48,768]{1,0:T(8,128)(2,1)S(1)}, bf16[48,768]{1,0:T(8,128)(2,1)S(1)}, u32[]{:S(2)}, u32[]{:S(2)}) collective-permute-start(bf16[48,768]{1,0:T(8,128)(2,1)S(1)} %fusion.63), channel_id=1, source_target_pairs={{0,128},{64,192},{128,0},{192,64},{1,129},{65,193},{129,1},{193,65... | collective-permute-start | bytes 221192 | tf_op jit(solution)/shard_map/ppermute | solution.py:15
  222.6 7.2 %collective-permute-start.34 = (bf16[48,768]{1,0:T(8,128)(2,1)S(1)}, bf16[48,768]{1,0:T(8,128)(2,1)S(1)}, u32[]{:S(2)}, u32[]{:S(2)}) collective-permute-start(bf16[48,768]{1,0:T(8,128)(2,1)S(1)} %add_convert_fusion.4), channel_id=1, source_target_pairs={{0,32},{32,0},{1,33},{33,1},{2,34},{34,2},{3,35},{35,3},{4,36},{36... | collective-permute-start | bytes 221192 | tf_op jit(solution)/shard_map/ppermute | solution.py:15
  229.8 3.3 %collective-permute-start.35 = (f32[48,768]{1,0:T(8,128)S(1)}, f32[48,768]{1,0:T(8,128)S(1)}, u32[]{:S(2)}, u32[]{:S(2)}) collective-permute-start(f32[48,768]{1,0:T(8,128)S(1)} %convert_add_fusion.4), channel_id=1, source_target_pairs={{0,16},{16,0},{1,17},{17,1},{2,18},{18,2},{3,19},{19,3},{4,20},{20... | collective-permute-start | bytes 442376 | tf_op jit(solution)/shard_map/ppermute | solution.py:15
  (3 other events, 2.3 us)

commit v2 on v1

--- a/solution.py
+++ b/solution.py
@@ -148,12 +148,10 @@
 
 
 def reflect_kernel(
-    padded_ref, gain_ref, own_ref, perm_ref, taps_hbm, out_hbm, wide_ref, narrow_ref,
+    edge_ref, rows_ref, gain_ref, own_ref, perm_ref, taps_hbm, out_hbm, wide_ref, narrow_ref,
     taps_ref, out_ref, hidden_ref, active_ref, partner_ref, mirror_ref, sems,
 ):
     count, channels = own_ref.shape
-    edge_ref = padded_ref.at[: 2 * DILATION_STEP, :]
-    rows_ref = padded_ref.at[2 * DILATION_STEP :, :]
 
     def put(cut, total):
         active_ref[:, cut] = narrow(gelu(total))
@@ -184,7 +182,7 @@
     narrow_ref[...] = narrow(wide_ref[...])
 
 
-def reflect(padded, norm_gain, block_out, rc_perm, taps, out_weight):
+def reflect(edges, rows, norm_gain, block_out, rc_perm, taps, out_weight):
     count, channels = block_out.shape
     vmem = pl.BlockSpec(memory_space=pltpu.VMEM)
     bf = jnp.bfloat16
@@ -194,7 +192,7 @@
             jax.ShapeDtypeStruct((count, channels), jnp.float32),
             jax.ShapeDtypeStruct((count, channels), bf),
         ],
-        in_specs=[vmem] * 4 + [pl.BlockSpec(memory_space=pltpu.HBM)] * 2,
+        in_specs=[vmem] * 5 + [pl.BlockSpec(memory_space=pltpu.HBM)] * 2,
         out_specs=[vmem] * 2,
         scratch_shapes=[
             pltpu.VMEM(taps.shape, bf),
@@ -214,7 +212,8 @@
         name="reflect",
         interpret=INTERPRET,
     )(
-        padded,
+        edges,
+        rows,
         norm_gain[None, :],
         block_out,
         rc_perm[None, :],
@@ -347,15 +346,12 @@
     rows = features[0]
     count_of_rows, channels = rows.shape
     low, high = edge_rows(rows, DILATION_STEP)
+    mirroring = [(i, bin_devices - 1 - i) for i in range(bin_devices)]
+    partner = lax.ppermute(rows, BINS, mirroring)
     head = gather_head(head_weight)
     entry_bins = listed_bins(exon_bins[0], exon_count[0])
     entries = entry_bins.size
     edges = jnp.concatenate([low, high], axis=0)
-    partner = lax.ppermute(
-        jnp.concatenate([edges, rows], axis=0),
-        BINS,
-        [(i, bin_devices - 1 - i) for i in range(bin_devices)],
-    )
     kept, sent, active, block_out, convolved_sum = forward(
         edges,
         rows,
@@ -371,6 +367,7 @@
     pieces = [shifted(pick(sent, (y + k) % ny), "y", k) for k in range(1, ny)]
     sent = narrow(wide(pick(sent, y)) + sum(wide(piece) for piece in pieces))
     sent = sent.reshape(nh, -1, kept.shape[1])
+    partner_edges = lax.ppermute(after(edges, kept), BINS, mirroring)
     piece = shifted(pick(sent, 1 - zh), "zh", 1)
     sent = narrow(wide(pick(sent, zh)) + wide(piece))
     distant_bins = by_distance(after(entry_bins, block_out))
@@ -392,6 +389,7 @@
     gathered_active = jnp.concatenate([piece[:sent_rows, channels:] for piece in pieces], axis=0)
     targets = wide(jnp.concatenate([piece[sent_rows:] for piece in pieces], axis=0))
     rc_grad, rc_narrow = reflect(
+        partner_edges,
         partner,
         norm_gain,
         block_out,
@@ -442,10 +440,9 @@
     share = narrow(share).reshape(nz, -1, half)
     pieces = [shifted(pick(share, (zl + k) % nz), "zl", k) for k in range(1, nz)]
     share = narrow(wide(pick(share, zl)) + sum(wide(piece) for piece in pieces))
-    share = narrow(
-        (wide(share) + wide(shifted(share, "y", 2)))
-        + (wide(shifted(share, "y", 1)) + wide(shifted(share, "y", 3)))
-    )
+    for flip in (1, 2):
+        piece = lax.ppermute(share, "y", [(i, i ^ flip) for i in range(ny)])
+        share = narrow(wide(share) + wide(piece))
     share = wide(share) + wide(shifted(share, "zh", 1))
     other = shifted(share, "core", 1)
     out_weight_grad = jnp.concatenate(

time: 235 us -> 201 us (0.86)
  starting transfers between devices: 95.8 us -> 82.7 us
  waiting for transfers between devices: 76.3 us -> 66 us
  other arithmetic: 13.9 us -> 7.02 us
  local copies, waits for them, and re-layouts: 13 us -> 8.35 us
    ppermute x1 -> x4, waiting for transfers between devices: 29.4 us -> 11.8 us  [the longest x1 9.25 us: whole_step(): partner_edges = lax.ppermute(after(edges, kept), BINS, mirroring)]
    ppermute x31 -> x28, starting transfers between devices: 60.1 us -> 49.9 us  [shifted(): lax.ppermute(block, axis, [(i, (i + shift) % count) for i in range(count)])]
    ppermute x31 -> x28, waiting for transfers between devices: 46.8 us -> 54.1 us  [shifted(): lax.ppermute(block, axis, [(i, (i + shift) % count) for i in range(count)])]
    ppermute x1 -> x4, starting transfers between devices: 14.3 us -> 11.5 us  [the longest x1 4.85 us: whole_step(): partner_edges = lax.ppermute(after(edges, kept), BINS, mirroring)]
    unnamed x35 -> x30, local copies, waits for them, and re-layouts: 4.99 us -> 4.66 us
  transfers between devices with their start and end apart: 36 -> 36, of which waited for: 14 -> 15; matrix products, arithmetic and copies ran while one was open for 12% -> 9% of each run, Pallas kernels for 9% -> 11%
where the time goes in v2:
time: 201 us; the launch traced here: 200 us
  starting transfers between devices  82.7 us (41%)
  waiting for transfers between devices  66 us (33%)
  Pallas kernels  22.8 us (11%)
  matrix products  11.8 us (6%)
  local copies, waits for them, and re-layouts  8.35 us (4%)
  other arithmetic  7.02 us (3%)
    ppermute x28, waiting for transfers between devices, shifted(): lax.ppermute(block, axis, [(i, (i + shift) % count) for i in range(count)])  54.1 us
    ppermute x28, starting transfers between devices, shifted(): lax.ppermute(block, axis, [(i, (i + shift) % count) for i in range(count)])  49.9 us
    ppermute x2, starting transfers between devices, edge_rows(): lax.ppermute(block[-width:], BINS, [(i, i + 1) for i in range(count - 1)])  14.8 us
    pallas_call x1, Pallas kernels, reflect(): pl.pallas_call(reflect_kernel, out_shape=[jax.ShapeDtypeStruct((count, ch...  12.4 us
    dot_general x12, matrix products, dot(): lax.dot_general(left, right, (((over[0],), (over[1],)), ((), ())), prefer...  11.8 us
    pallas_call x1, Pallas kernels, forward(): pl.pallas_call(forward_kernel, out_shape=[payload, payload, jax.ShapeDtyp...  10.5 us
    ppermute x1, waiting for transfers between devices, whole_step(): partner_edges = lax.ppermute(after(edges, kept), BINS, mirroring)  9.25 us
    ppermute x2, starting transfers between devices, edge_rows(): lax.ppermute(block[:width], BINS, [(i + 1, i) for i in range(count - 1)])  6.46 us
  transfers between devices with their start and end apart: 36, of which 15 were waited for; matrix products, arithmetic and copies ran while one was open for 9% of the time, Pallas kernels for 11%

profile of v2, /device:TPU:1, one launch (start us, length us, event | category | flops | bytes accessed | tf_op | source)
XLA Modules:
  0.0 200.2 jit_solution(6082994571673487325)
XLA Ops:
  0.6 3.4 %collective-permute-start.12 = (bf16[256,1536]{0,1:T(8,128)(2,1)}, bf16[256,1536]{0,1:T(8,128)(2,1)}, u32[]{:S(2)}, u32[]{:S(2)}) collective-permute-start(bf16[256,1536]{0,1:T(8,128)(2,1)} %bitcast.132), channel_id=1, source_target_pairs={{0,12},{4,0},{8,4},{12,8},{1,13},{5,1},{9,5},{13,9},{2,14},{6,2},{... | collective-permute-start | bytes 2359304 | tf_op jit(solution)/shard_map/ppermute | solution.py:15
  5.4 3.1 %collective-permute-start.1 = (bf16[16,1536]{1,0:T(8,128)(2,1)S(1)}, bf16[16,1536]{1,0:T(8,128)(2,1)S(1)}, u32[]{:S(2)}, u32[]{:S(2)}) collective-permute-start(bf16[16,1536]{1,0:T(8,128)(2,1)S(1)} %get-tuple-element.38), channel_id=1, source_target_pairs={{16,0},{32,16},{48,32},{64,48},{80,64},{96,80},{112,96},{128,112},... | collective-permute-start | bytes 147464 | tf_op jit(solution)/shard_map/ppermute | solution.py:21
  8.5 8.7 %collective-permute-start = (bf16[16,1536]{1,0:T(8,128)(2,1)S(1)}, bf16[16,1536]{1,0:T(8,128)(2,1)S(1)}, u32[]{:S(2)}, u32[]{:S(2)}) collective-permute-start(bf16[16,1536]{1,0:T(8,128)(2,1)S(1)} %get-tuple-element.39), channel_id=1, source_target_pairs={{0,16},{16,32},{32,48},{48,64},{64,80},{80,96},{96,112},{112,128},... | collective-permute-start | bytes 147464 | tf_op jit(solution)/shard_map/ppermute | solution.py:20
  17.2 3.0 %collective-permute-start.22 = (bf16[256,1536]{1,0:T(8,128)(2,1)}, bf16[256,1536]{1,0:T(8,128)(2,1)}, u32[]{:S(2)}, u32[]{:S(2)}) collective-permute-start(bf16[256,1536]{1,0:T(8,128)(2,1)} %bitcast.112), channel_id=1, source_target_pairs={{0,240},{16,224},{32,208},{48,192},{64,176},{80,160},{96,144},{112... | collective-permute-start | bytes 2359304 | tf_op jit(solution)/shard_map/ppermute | solution.py:350
  21.8 1.3 reduce.5
  26.0 1.1 copy-done
  27.1 10.5 %forward.1 = (bf16[256,2304]{1,0:T(8,128)(2,1)S(1)}, bf16[256,2304]{1,0:T(8,128)(2,1)S(1)}, bf16[256,768]{1,0:T(8,128)(2,1)S(1)}, bf16[256,1536]{1,0:T(8,128)(2,1)}, f32[256,768]{1,0:T(8,128)}) custom-call(s32[2]{0:T(128)S(1)} %pad_add_fusion.base_ref, bf16[32,1536]{1,0:T(8,128)(2,1)S(1)} %constant_dynamic-update-slice_fusion.edge_ref, ...), custom_call_target="tpu_custom_call" | custom-call | flops 3019898880 | bytes 12582912 | tf_op jit(solution)/shard_map/forward/pallas_call | solution.py:240
  38.5 4.8 %collective-permute-start.21 = (bf16[32,1536]{1,0:T(8,128)(2,1)S(1)}, bf16[32,1536]{1,0:T(8,128)(2,1)S(1)}, u32[]{:S(2)}, u32[]{:S(2)}) collective-permute-start(bf16[32,1536]{1,0:T(8,128)(2,1)S(1)} %constant_dynamic-update-slice_fusion.edge_ref), channel_id=1, source_target_pairs={{0,240},{16,224},{32,208},{48,192},{64,176},{80,160},{96,144},{112... | collective-permute-start | bytes 294920 | tf_op jit(solution)/shard_map/ppermute | solution.py:370
  43.9 2.4 %collective-permute-done.2 = bf16[256,2304]{1,0:T(8,128)(2,1)S(1)} collective-permute-done((bf16[256,2304]{1,0:T(8,128)(2,1)S(1)}, bf16[256,2304]{1,0:T(8,128)(2,1)S(1)}, u32[]{:S(2)}, u32[]{:S(2)}) %collective-permute-start.2) | collective-permute-done | bytes 1179680 | tf_op jit(solution)/shard_map/ppermute | solution.py:15
  46.8 9.2 %collective-permute-done.21.edge_ref = bf16[32,1536]{1,0:T(8,128)(2,1)S(1)} collective-permute-done((bf16[32,1536]{1,0:T(8,128)(2,1)S(1)}, bf16[32,1536]{1,0:T(8,128)(2,1)S(1)}, u32[]{:S(2)}, u32[]{:S(2)}) %collective-permute-start.21) | collective-permute-done | bytes 98336 | tf_op jit(solution)/shard_map/ppermute | solution.py:370
  56.0 10.0 %collective-permute-start.5 = (bf16[64,2304]{1,0:T(8,128)(2,1)S(1)}, bf16[64,2304]{1,0:T(8,128)(2,1)S(1)}, u32[]{:S(2)}, u32[]{:S(2)}) collective-permute-start(bf16[64,2304]{1,0:T(8,128)(2,1)S(1)} %get-tuple-element.34), channel_id=1, source_target_pairs={{0,192},{64,0},{128,64},{192,128},{1,193},{65,1},{129,65},{193,129... | collective-permute-start | bytes 884744 | tf_op jit(solution)/shard_map/ppermute | solution.py:15
  66.0 12.4 %reflect.1 = (f32[256,1536]{1,0:T(8,128)S(1)}, bf16[256,1536]{1,0:T(8,128)(2,1)S(1)}) custom-call(bf16[32,1536]{1,0:T(8,128)(2,1)S(1)} %collective-permute-done.21.edge_ref, bf16[256,1536]{1,0:T(8,128)(2,1)} %collective-permute-done.22.rows_ref, f32[1,1536]{1,0:T(1,128)S(1)} %broadcast_in_dim.77.gain_ref, bf16[256,1536]{1,0:T(8,128)(2,1)S(1)} %copy-done.2, ...), custom_call_target="tpu_custom_call" | custom-call | flops 4831838208 | bytes 13369344 | tf_op jit(solution)/shard_map/reflect/pallas_call | solution.py:189
  79.5 12.8 %collective-permute-done.6 = bf16[32,2304]{1,0:T(8,128)(2,1)S(1)} collective-permute-done((bf16[32,2304]{1,0:T(8,128)(2,1)S(1)}, bf16[32,2304]{1,0:T(8,128)(2,1)S(1)}, u32[]{:S(2)}, u32[]{:S(2)}) %collective-permute-start.6) | collective-permute-done | bytes 147488 | tf_op jit(solution)/shard_map/ppermute | solution.py:15
  92.4 0.9 collective-permute-start.7
  94.2 6.1 %collective-permute-done.7 = bf16[36,2304]{1,0:T(8,128)(2,1)S(1)} collective-permute-done((bf16[36,2304]{1,0:T(8,128)(2,1)S(1)}, bf16[36,2304]{1,0:T(8,128)(2,1)S(1)}, u32[]{:S(2)}, u32[]{:S(2)}) %collective-permute-start.7) | collective-permute-done | bytes 165920 | tf_op jit(solution)/shard_map/ppermute | solution.py:15
  100.9 8.0 %collective-permute-done.8 = bf16[36,2304]{1,0:T(8,128)(2,1)S(1)} collective-permute-done((bf16[36,2304]{1,0:T(8,128)(2,1)S(1)}, bf16[36,2304]{1,0:T(8,128)(2,1)S(1)}, u32[]{:S(2)}, u32[]{:S(2)}) %collective-permute-start.8) | collective-permute-done | bytes 165920 | tf_op jit(solution)/shard_map/ppermute | solution.py:15
  109.3 2.3 %fusion.38 = (f32[16,1024]{1,0:T(8,128)S(1)}, f32[128,1024]{1,0:T(8,128)S(1)}) fusion(pred[16,8]{1,0:T(8,128)(4,1)S(1)} %iota_compare_fusion, bf16[256,1536]{0,1:T(8,128)(2,1)} %collective-permute-done.12, bf16[256,1536]{0,1:T(8,128)(2,1)} %collective-permute-done.11, bf16[256,1536]{0,1:T(8,128)(2,1)S(1)} %collective-permute-done.10, ...), kind=kOutput, calls=%fused_computation.57 | convolution fusion | flops 418103296 | bytes 4128896 | tf_op jit(solution)/shard_map/dot_general | solution.py:45
  111.7 2.6 %convolution_convert_fusion = bf16[128,1536]{1,0:T(8,128)(2,1)S(1)} fusion(bf16[256,1536]{0,1:T(8,128)(2,1)} %collective-permute-done.12, bf16[256,1536]{0,1:T(8,128)(2,1)} %collective-permute-done.11, bf16[256,1536]{0,1:T(8,128)(2,1)S(1)} %collective-permute-done.10, bf16[256,1536]{0,1:T(8,128)(2,1)S(1)} %bitcast.136, ...), kind=kOutput, calls=%fused_computation.12 | convolution fusion | flops 416088064 | bytes 4128768 | tf_op jit(solution)/shard_map/dot_general | solution.py:45
  114.4 3.3 %collective-permute-start.13 = (bf16[32,1536]{1,0:T(8,128)(2,1)S(1)}, bf16[32,1536]{1,0:T(8,128)(2,1)S(1)}, u32[]{:S(2)}, u32[]{:S(2)}) collective-permute-start(bf16[32,1536]{1,0:T(8,128)(2,1)S(1)} %get-tuple-element.44), channel_id=1, source_target_pairs={{0,3},{1,0},{2,1},{3,2},{4,7},{5,4},{6,5},{7,6},{8,11},{9,8},{10,9... | collective-permute-start | bytes 294920 | tf_op jit(solution)/shard_map/ppermute | solution.py:15
  119.3 3.8 %collective-permute-done.15 = bf16[32,1536]{1,0:T(8,128)(2,1)S(1)} collective-permute-done((bf16[32,1536]{1,0:T(8,128)(2,1)S(1)}, bf16[32,1536]{1,0:T(8,128)(2,1)S(1)}, u32[]{:S(2)}, u32[]{:S(2)}) %collective-permute-start.15) | collective-permute-done | bytes 98336 | tf_op jit(solution)/shard_map/ppermute | solution.py:15
  123.1 1.0 collective-permute-done.14
  125.4 5.6 %collective-permute-start.25 = (bf16[768,768]{1,0:T(8,128)(2,1)S(1)}, bf16[768,768]{1,0:T(8,128)(2,1)S(1)}, u32[]{:S(2)}, u32[]{:S(2)}) collective-permute-start(bf16[768,768]{1,0:T(8,128)(2,1)S(1)} %add_convert_fusion.1), channel_id=1, source_target_pairs={{0,16},{16,0},{1,17},{17,1},{2,18},{18,2},{3,19},{19,3},{4,20},{20... | collective-permute-start | bytes 3538952 | tf_op jit(solution)/shard_map/ppermute | solution.py:15
  131.1 1.0 collective-permute-done.16
  132.2 1.8 collective-permute-start.18
  134.0 1.7 collective-permute-start.17
  135.7 4.8 %collective-permute-done.17 = bf16[64,1536]{1,0:T(8,128)(2,1)S(1)} collective-permute-done((bf16[64,1536]{1,0:T(8,128)(2,1)S(1)}, bf16[64,1536]{1,0:T(8,128)(2,1)S(1)}, u32[]{:S(2)}, u32[]{:S(2)}) %collective-permute-start.17) | collective-permute-done | bytes 196640 | tf_op jit(solution)/shard_map/ppermute | solution.py:15
  140.6 7.3 %collective-permute-start.20 = (bf16[256,1536]{1,0:T(8,128)(2,1)S(1)}, bf16[256,1536]{1,0:T(8,128)(2,1)S(1)}, u32[]{:S(2)}, u32[]{:S(2)}) collective-permute-start(bf16[256,1536]{1,0:T(8,128)(2,1)S(1)} %constant_dynamic-update-slice_fusion.2), channel_id=1, source_target_pairs={{0,16},{16,0},{1,17},{17,1},{2,18},{18,2},{3,19},{19,3},{4,20},{20... | collective-permute-start | bytes 2359304 | tf_op jit(solution)/shard_map/ppermute | solution.py:15
  149.0 1.8 collective-permute-start.26
  150.8 1.2 collective-permute-start.28
  151.9 1.1 collective-permute-start.27
  153.8 0.8 copy-done.6
  154.7 0.9 fusion.28
  155.9 0.9 slice-done.1
  157.7 1.3 collective-permute-done.26
  159.0 6.8 %collective-permute-done.27 = bf16[192,768]{1,0:T(8,128)(2,1)S(1)} collective-permute-done((bf16[192,768]{1,0:T(8,128)(2,1)S(1)}, bf16[192,768]{1,0:T(8,128)(2,1)S(1)}, u32[]{:S(2)}, u32[]{:S(2)}) %collective-permute-start.27) | collective-permute-done | bytes 294944 | tf_op jit(solution)/shard_map/ppermute | solution.py:15
  166.1 1.3 collective-permute-start.29
  167.4 2.8 %collective-permute-start.31 = (bf16[48,768]{1,0:T(8,128)(2,1)S(1)}, bf16[48,768]{1,0:T(8,128)(2,1)S(1)}, u32[]{:S(2)}, u32[]{:S(2)}) collective-permute-start(bf16[48,768]{1,0:T(8,128)(2,1)S(1)} %get-tuple-element.50), channel_id=1, source_target_pairs={{0,3},{1,0},{2,1},{3,2},{4,7},{5,4},{6,5},{7,6},{8,11},{9,8},{10,9... | collective-permute-start | bytes 221192 | tf_op jit(solution)/shard_map/ppermute | solution.py:15
  170.3 3.3 %collective-permute-start.23 = (bf16[16,768]{1,0:T(8,128)(2,1)S(1)}, bf16[16,768]{1,0:T(8,128)(2,1)S(1)}, u32[]{:S(2)}, u32[]{:S(2)}) collective-permute-start(bf16[16,768]{1,0:T(8,128)(2,1)S(1)} %get-tuple-element.42), channel_id=1, source_target_pairs={{16,0},{32,16},{48,32},{64,48},{80,64},{96,80},{112,96},{128,112},... | collective-permute-start | bytes 73736 | tf_op jit(solution)/shard_map/ppermute | solution.py:21
  173.7 6.1 %collective-permute-start.24 = (bf16[16,768]{1,0:T(8,128)(2,1)S(1)}, bf16[16,768]{1,0:T(8,128)(2,1)S(1)}, u32[]{:S(2)}, u32[]{:S(2)}) collective-permute-start(bf16[16,768]{1,0:T(8,128)(2,1)S(1)} %get-tuple-element.43), channel_id=1, source_target_pairs={{0,16},{16,32},{32,48},{48,64},{64,80},{80,96},{96,112},{112,128},... | collective-permute-start | bytes 73736 | tf_op jit(solution)/shard_map/ppermute | solution.py:20
  179.9 1.4 collective-permute-start.32
  182.2 1.0 collective-permute-done.32
  183.2 2.2 %collective-permute-start.33 = (bf16[48,768]{1,0:T(8,128)(2,1)S(1)}, bf16[48,768]{1,0:T(8,128)(2,1)S(1)}, u32[]{:S(2)}, u32[]{:S(2)}) collective-permute-start(bf16[48,768]{1,0:T(8,128)(2,1)S(1)} %add_convert_fusion.5), channel_id=1, source_target_pairs={{0,128},{64,192},{128,0},{192,64},{1,129},{65,193},{129,1},{193,65... | collective-permute-start | bytes 221192 | tf_op jit(solution)/shard_map/ppermute | solution.py:444
  185.4 1.6 fusion.27
  187.0 1.6 collective-permute-done.33
  188.6 2.0 collective-permute-start.34
  190.6 5.3 %collective-permute-done.34 = bf16[48,768]{1,0:T(8,128)(2,1)S(1)} collective-permute-done((bf16[48,768]{1,0:T(8,128)(2,1)S(1)}, bf16[48,768]{1,0:T(8,128)(2,1)S(1)}, u32[]{:S(2)}, u32[]{:S(2)}) %collective-permute-start.34) | collective-permute-done | bytes 73760 | tf_op jit(solution)/shard_map/ppermute | solution.py:15
  195.9 2.2 %collective-permute-start.35 = (f32[48,768]{1,0:T(8,128)S(1)}, f32[48,768]{1,0:T(8,128)S(1)}, u32[]{:S(2)}, u32[]{:S(2)}) collective-permute-start(f32[48,768]{1,0:T(8,128)S(1)} %convert_add_fusion.4), channel_id=1, source_target_pairs={{0,16},{16,0},{1,17},{17,1},{2,18},{18,2},{3,19},{19,3},{4,20},{20... | collective-permute-start | bytes 442376 | tf_op jit(solution)/shard_map/ppermute | solution.py:15
  198.1 1.3 fusion.33
  (148 shorter events, 18.5 us)
Async XLA Ops:
  0.6 108.7 %collective-permute-start.12 = (bf16[256,1536]{0,1:T(8,128)(2,1)}, bf16[256,1536]{0,1:T(8,128)(2,1)}, u32[]{:S(2)}, u32[]{:S(2)}) collective-permute-start(bf16[256,1536]{0,1:T(8,128)(2,1)} %bitcast.132), channel_id=1, source_target_pairs={{0,12},{4,0},{8,4},{12,8},{1,13},{5,1},{9,5},{13,9},{2,14},{6,2},{... | collective-permute-start | bytes 2359304 | tf_op jit(solution)/shard_map/ppermute | solution.py:15
  4.0 105.3 %collective-permute-start.11 = (bf16[256,1536]{0,1:T(8,128)(2,1)}, bf16[256,1536]{0,1:T(8,128)(2,1)}, u32[]{:S(2)}, u32[]{:S(2)}) collective-permute-start(bf16[256,1536]{0,1:T(8,128)(2,1)} %bitcast.133), channel_id=1, source_target_pairs={{0,8},{4,12},{8,0},{12,4},{1,9},{5,13},{9,1},{13,5},{2,10},{6,14},... | collective-permute-start | bytes 2359304 | tf_op jit(solution)/shard_map/ppermute | solution.py:15
  5.4 20.6 %collective-permute-start.1 = (bf16[16,1536]{1,0:T(8,128)(2,1)S(1)}, bf16[16,1536]{1,0:T(8,128)(2,1)S(1)}, u32[]{:S(2)}, u32[]{:S(2)}) collective-permute-start(bf16[16,1536]{1,0:T(8,128)(2,1)S(1)} %get-tuple-element.38), channel_id=1, source_target_pairs={{16,0},{32,16},{48,32},{64,48},{80,64},{96,80},{112,96},{128,112},... | collective-permute-start | bytes 147464 | tf_op jit(solution)/shard_map/ppermute | solution.py:21
  8.5 17.5 %collective-permute-start = (bf16[16,1536]{1,0:T(8,128)(2,1)S(1)}, bf16[16,1536]{1,0:T(8,128)(2,1)S(1)}, u32[]{:S(2)}, u32[]{:S(2)}) collective-permute-start(bf16[16,1536]{1,0:T(8,128)(2,1)S(1)} %get-tuple-element.39), channel_id=1, source_target_pairs={{0,16},{16,32},{32,48},{48,64},{64,80},{80,96},{96,112},{112,128},... | collective-permute-start | bytes 147464 | tf_op jit(solution)/shard_map/ppermute | solution.py:20
  17.2 48.8 %collective-permute-start.22 = (bf16[256,1536]{1,0:T(8,128)(2,1)}, bf16[256,1536]{1,0:T(8,128)(2,1)}, u32[]{:S(2)}, u32[]{:S(2)}) collective-permute-start(bf16[256,1536]{1,0:T(8,128)(2,1)} %bitcast.112), channel_id=1, source_target_pairs={{0,240},{16,224},{32,208},{48,192},{64,176},{80,160},{96,144},{112... | collective-permute-start | bytes 2359304 | tf_op jit(solution)/shard_map/ppermute | solution.py:350
  26.0 1.1 copy-start
  27.1 10.5 %copy-start.3 = (f32[1,4,4096]{2,1,0:T(4,128)S(1)}, f32[1,4,4096]{2,1,0:T(4,128)}, u32[]{:S(2)}) copy-start(f32[1,4,4096]{2,1,0:T(4,128)} %param.19) | copy-start | bytes 196612
  27.1 10.6 %copy-start.8 = (s32[1,64]{1,0:T(1,128)S(1)}, s32[1,64]{1,0:T(1,128)}, u32[]{:S(2)}) copy-start(s32[1,64]{1,0:T(1,128)} %param.18) | copy-start | bytes 772
  27.1 10.7 %copy-start.5 = (s32[1,64]{1,0:T(1,128)S(1)}, s32[1,64]{1,0:T(1,128)}, u32[]{:S(2)}) copy-start(s32[1,64]{1,0:T(1,128)} %param.17) | copy-start | bytes 772
  38.5 17.5 %collective-permute-start.21 = (bf16[32,1536]{1,0:T(8,128)(2,1)S(1)}, bf16[32,1536]{1,0:T(8,128)(2,1)S(1)}, u32[]{:S(2)}, u32[]{:S(2)}) collective-permute-start(bf16[32,1536]{1,0:T(8,128)(2,1)S(1)} %constant_dynamic-update-slice_fusion.edge_ref), channel_id=1, source_target_pairs={{0,240},{16,224},{32,208},{48,192},{64,176},{80,160},{96,144},{112... | collective-permute-start | bytes 294920 | tf_op jit(solution)/shard_map/ppermute | solution.py:370
  43.4 2.8 %collective-permute-start.2 = (bf16[256,2304]{1,0:T(8,128)(2,1)S(1)}, bf16[256,2304]{1,0:T(8,128)(2,1)S(1)}, u32[]{:S(2)}, u32[]{:S(2)}) collective-permute-start(bf16[256,2304]{1,0:T(8,128)(2,1)S(1)} %get-tuple-element.21), channel_id=1, source_target_pairs={{0,16},{16,0},{1,17},{17,1},{2,18},{18,2},{3,19},{19,3},{4,20},{20... | collective-permute-start | bytes 3538952 | tf_op jit(solution)/shard_map/ppermute | solution.py:15
  46.5 19.5 %copy-start.2 = (bf16[256,1536]{1,0:T(8,128)(2,1)S(1)}, bf16[256,1536]{1,0:T(8,128)(2,1)}, u32[]{:S(2)}) copy-start(bf16[256,1536]{1,0:T(8,128)(2,1)} %get-tuple-element.15.own_ref) | copy-start | bytes 2359300
  46.6 31.8 %collective-permute-start.3 = (bf16[64,2304]{1,0:T(8,128)(2,1)S(1)}, bf16[64,2304]{1,0:T(8,128)(2,1)S(1)}, u32[]{:S(2)}, u32[]{:S(2)}) collective-permute-start(bf16[64,2304]{1,0:T(8,128)(2,1)S(1)} %get-tuple-element.33), channel_id=1, source_target_pairs={{0,64},{64,128},{128,192},{192,0},{1,65},{65,129},{129,193},{193,1... | collective-permute-start | bytes 884744 | tf_op jit(solution)/shard_map/ppermute | solution.py:15
  56.0 23.1 %collective-permute-start.5 = (bf16[64,2304]{1,0:T(8,128)(2,1)S(1)}, bf16[64,2304]{1,0:T(8,128)(2,1)S(1)}, u32[]{:S(2)}, u32[]{:S(2)}) collective-permute-start(bf16[64,2304]{1,0:T(8,128)(2,1)S(1)} %get-tuple-element.34), channel_id=1, source_target_pairs={{0,192},{64,0},{128,64},{192,128},{1,193},{65,1},{129,65},{193,129... | collective-permute-start | bytes 884744 | tf_op jit(solution)/shard_map/ppermute | solution.py:15
  66.0 12.4 %copy-start.7 = (bf16[1536,256]{1,0:T(8,128)(2,1)S(1)}, bf16[1536,256]{1,0:T(8,128)(2,1)}, u32[]{:S(2)}) copy-start(bf16[1536,256]{1,0:T(8,128)(2,1)} %param.14) | copy-start | bytes 2359300
  66.0 13.1 %collective-permute-start.4 = (bf16[64,2304]{1,0:T(8,128)(2,1)S(1)}, bf16[64,2304]{1,0:T(8,128)(2,1)S(1)}, u32[]{:S(2)}, u32[]{:S(2)}) collective-permute-start(bf16[64,2304]{1,0:T(8,128)(2,1)S(1)} %get-tuple-element.35), channel_id=1, source_target_pairs={{0,128},{64,192},{128,0},{192,64},{1,129},{65,193},{129,1},{193,65... | collective-permute-start | bytes 884744 | tf_op jit(solution)/shard_map/ppermute | solution.py:15
  78.4 30.9 %collective-permute-start.10 = (bf16[256,1536]{0,1:T(8,128)(2,1)S(1)}, bf16[256,1536]{0,1:T(8,128)(2,1)S(1)}, u32[]{:S(2)}, u32[]{:S(2)}) collective-permute-start(bf16[256,1536]{0,1:T(8,128)(2,1)S(1)} %bitcast.134), channel_id=1, source_target_pairs={{0,4},{4,8},{8,12},{12,0},{1,5},{5,9},{9,13},{13,1},{2,6},{6,10},{... | collective-permute-start | bytes 2359304 | tf_op jit(solution)/shard_map/ppermute | solution.py:15
  79.3 13.0 %collective-permute-start.6 = (bf16[32,2304]{1,0:T(8,128)(2,1)S(1)}, bf16[32,2304]{1,0:T(8,128)(2,1)S(1)}, u32[]{:S(2)}, u32[]{:S(2)}) collective-permute-start(bf16[32,2304]{1,0:T(8,128)(2,1)S(1)} %dynamic-slice_bitcast_fusion.6), channel_id=1, source_target_pairs={{0,32},{32,0},{1,33},{33,1},{2,34},{34,2},{3,35},{35,3},{4,36},{36... | collective-permute-start | bytes 442376 | tf_op jit(solution)/shard_map/ppermute | solution.py:15
  92.4 7.9 %collective-permute-start.7 = (bf16[36,2304]{1,0:T(8,128)(2,1)S(1)}, bf16[36,2304]{1,0:T(8,128)(2,1)S(1)}, u32[]{:S(2)}, u32[]{:S(2)}) collective-permute-start(bf16[36,2304]{1,0:T(8,128)(2,1)S(1)} %get-tuple-element.52), channel_id=1, source_target_pairs={{0,1},{1,2},{2,3},{3,0},{4,5},{5,6},{6,7},{7,4},{8,9},{9,10},{10,1... | collective-permute-start | bytes 497672 | tf_op jit(solution)/shard_map/ppermute | solution.py:15
  93.5 15.4 %collective-permute-start.8 = (bf16[36,2304]{1,0:T(8,128)(2,1)S(1)}, bf16[36,2304]{1,0:T(8,128)(2,1)S(1)}, u32[]{:S(2)}, u32[]{:S(2)}) collective-permute-start(bf16[36,2304]{1,0:T(8,128)(2,1)S(1)} %get-tuple-element.53), channel_id=1, source_target_pairs={{0,2},{1,3},{2,0},{3,1},{4,6},{5,7},{6,4},{7,5},{8,10},{9,11},{10,... | collective-permute-start | bytes 497672 | tf_op jit(solution)/shard_map/ppermute | solution.py:15
  100.3 8.7 %collective-permute-start.9 = (bf16[36,2304]{1,0:T(8,128)(2,1)S(1)}, bf16[36,2304]{1,0:T(8,128)(2,1)S(1)}, u32[]{:S(2)}, u32[]{:S(2)}) collective-permute-start(bf16[36,2304]{1,0:T(8,128)(2,1)S(1)} %get-tuple-element.54), channel_id=1, source_target_pairs={{0,3},{1,0},{2,1},{3,2},{4,7},{5,4},{6,5},{7,6},{8,11},{9,8},{10,9... | collective-permute-start | bytes 497672 | tf_op jit(solution)/shard_map/ppermute | solution.py:15
  114.4 4.9 %collective-permute-start.13 = (bf16[32,1536]{1,0:T(8,128)(2,1)S(1)}, bf16[32,1536]{1,0:T(8,128)(2,1)S(1)}, u32[]{:S(2)}, u32[]{:S(2)}) collective-permute-start(bf16[32,1536]{1,0:T(8,128)(2,1)S(1)} %get-tuple-element.44), channel_id=1, source_target_pairs={{0,3},{1,0},{2,1},{3,2},{4,7},{5,4},{6,5},{7,6},{8,11},{9,8},{10,9... | collective-permute-start | bytes 294920 | tf_op jit(solution)/shard_map/ppermute | solution.py:15
  117.7 5.5 %collective-permute-start.15 = (bf16[32,1536]{1,0:T(8,128)(2,1)S(1)}, bf16[32,1536]{1,0:T(8,128)(2,1)S(1)}, u32[]{:S(2)}, u32[]{:S(2)}) collective-permute-start(bf16[32,1536]{1,0:T(8,128)(2,1)S(1)} %get-tuple-element.45), channel_id=1, source_target_pairs={{0,1},{1,2},{2,3},{3,0},{4,5},{5,6},{6,7},{7,4},{8,9},{9,10},{10,1... | collective-permute-start | bytes 294920 | tf_op jit(solution)/shard_map/ppermute | solution.py:15
  117.7 6.4 %collective-permute-start.14 = (bf16[32,1536]{1,0:T(8,128)(2,1)S(1)}, bf16[32,1536]{1,0:T(8,128)(2,1)S(1)}, u32[]{:S(2)}, u32[]{:S(2)}) collective-permute-start(bf16[32,1536]{1,0:T(8,128)(2,1)S(1)} %get-tuple-element.46), channel_id=1, source_target_pairs={{0,2},{1,3},{2,0},{3,1},{4,6},{5,7},{6,4},{7,5},{8,10},{9,11},{10,... | collective-permute-start | bytes 294920 | tf_op jit(solution)/shard_map/ppermute | solution.py:15
  124.2 7.9 %collective-permute-start.16 = (bf16[32,1536]{1,0:T(8,128)(2,1)S(1)}, bf16[32,1536]{1,0:T(8,128)(2,1)S(1)}, u32[]{:S(2)}, u32[]{:S(2)}) collective-permute-start(bf16[32,1536]{1,0:T(8,128)(2,1)S(1)} %get-tuple-element.29), channel_id=1, source_target_pairs={{0,32},{32,0},{1,33},{33,1},{2,34},{34,2},{3,35},{35,3},{4,36},{36... | collective-permute-start | bytes 294920 | tf_op jit(solution)/shard_map/ppermute | solution.py:15
  125.4 23.0 %collective-permute-start.25 = (bf16[768,768]{1,0:T(8,128)(2,1)S(1)}, bf16[768,768]{1,0:T(8,128)(2,1)S(1)}, u32[]{:S(2)}, u32[]{:S(2)}) collective-permute-start(bf16[768,768]{1,0:T(8,128)(2,1)S(1)} %add_convert_fusion.1), channel_id=1, source_target_pairs={{0,16},{16,0},{1,17},{17,1},{2,18},{18,2},{3,19},{19,3},{4,20},{20... | collective-permute-start | bytes 3538952 | tf_op jit(solution)/shard_map/ppermute | solution.py:15
  132.1 8.5 %collective-permute-start.19 = (bf16[64,1536]{1,0:T(8,128)(2,1)S(1)}, bf16[64,1536]{1,0:T(8,128)(2,1)S(1)}, u32[]{:S(2)}, u32[]{:S(2)}) collective-permute-start(bf16[64,1536]{1,0:T(8,128)(2,1)S(1)} %pad_maximum_fusion.8), channel_id=1, source_target_pairs={{0,64},{64,128},{128,192},{192,0},{1,65},{65,129},{129,193},{193,1... | collective-permute-start | bytes 589832 | tf_op jit(solution)/shard_map/ppermute | solution.py:15
  132.2 8.4 %collective-permute-start.18 = (bf16[64,1536]{1,0:T(8,128)(2,1)S(1)}, bf16[64,1536]{1,0:T(8,128)(2,1)S(1)}, u32[]{:S(2)}, u32[]{:S(2)}) collective-permute-start(bf16[64,1536]{1,0:T(8,128)(2,1)S(1)} %pad_maximum_fusion.8), channel_id=1, source_target_pairs={{0,128},{64,192},{128,0},{192,64},{1,129},{65,193},{129,1},{193,65... | collective-permute-start | bytes 589832 | tf_op jit(solution)/shard_map/ppermute | solution.py:15
  134.0 6.6 %collective-permute-start.17 = (bf16[64,1536]{1,0:T(8,128)(2,1)S(1)}, bf16[64,1536]{1,0:T(8,128)(2,1)S(1)}, u32[]{:S(2)}, u32[]{:S(2)}) collective-permute-start(bf16[64,1536]{1,0:T(8,128)(2,1)S(1)} %pad_maximum_fusion.8), channel_id=1, source_target_pairs={{0,192},{64,0},{128,64},{192,128},{1,193},{65,1},{129,65},{193,129... | collective-permute-start | bytes 589832 | tf_op jit(solution)/shard_map/ppermute | solution.py:15
  140.6 12.4 %collective-permute-start.20 = (bf16[256,1536]{1,0:T(8,128)(2,1)S(1)}, bf16[256,1536]{1,0:T(8,128)(2,1)S(1)}, u32[]{:S(2)}, u32[]{:S(2)}) collective-permute-start(bf16[256,1536]{1,0:T(8,128)(2,1)S(1)} %constant_dynamic-update-slice_fusion.2), channel_id=1, source_target_pairs={{0,16},{16,0},{1,17},{17,1},{2,18},{18,2},{3,19},{19,3},{4,20},{20... | collective-permute-start | bytes 2359304 | tf_op jit(solution)/shard_map/ppermute | solution.py:15
  148.9 5.0 %copy-start.9 = (f32[256,768]{1,0:T(8,128)S(1)}, f32[256,768]{1,0:T(8,128)}, u32[]{:S(2)}) copy-start(f32[256,768]{1,0:T(8,128)} %get-tuple-element.25) | copy-start | bytes 2359300
  149.0 10.1 %collective-permute-start.26 = (bf16[192,768]{1,0:T(8,128)(2,1)S(1)}, bf16[192,768]{1,0:T(8,128)(2,1)S(1)}, u32[]{:S(2)}, u32[]{:S(2)}) collective-permute-start(bf16[192,768]{1,0:T(8,128)(2,1)S(1)} %get-tuple-element.30), channel_id=1, source_target_pairs={{0,4},{4,8},{8,12},{12,0},{1,5},{5,9},{9,13},{13,1},{2,6},{6,10},{... | collective-permute-start | bytes 884744 | tf_op jit(solution)/shard_map/ppermute | solution.py:15
  150.8 8.3 %collective-permute-start.28 = (bf16[192,768]{1,0:T(8,128)(2,1)S(1)}, bf16[192,768]{1,0:T(8,128)(2,1)S(1)}, u32[]{:S(2)}, u32[]{:S(2)}) collective-permute-start(bf16[192,768]{1,0:T(8,128)(2,1)S(1)} %get-tuple-element.31), channel_id=1, source_target_pairs={{0,12},{4,0},{8,4},{12,8},{1,13},{5,1},{9,5},{13,9},{2,14},{6,2},{... | collective-permute-start | bytes 884744 | tf_op jit(solution)/shard_map/ppermute | solution.py:15
  151.9 13.9 %collective-permute-start.27 = (bf16[192,768]{1,0:T(8,128)(2,1)S(1)}, bf16[192,768]{1,0:T(8,128)(2,1)S(1)}, u32[]{:S(2)}, u32[]{:S(2)}) collective-permute-start(bf16[192,768]{1,0:T(8,128)(2,1)S(1)} %get-tuple-element.32), channel_id=1, source_target_pairs={{0,8},{4,12},{8,0},{12,4},{1,9},{5,13},{9,1},{13,5},{2,10},{6,14},... | collective-permute-start | bytes 884744 | tf_op jit(solution)/shard_map/ppermute | solution.py:15
  153.0 1.7 copy-start.6
  153.0 2.9 %slice-start = ((s8[7077888]{0:T(1024)(128)(4,1)}), s8[4194304]{0:T(1024)(128)(4,1)S(1)}, s32[]{:S(2)}) async-start(s8[7077888]{0:T(1024)(128)(4,1)} %bitcast.130), calls=%async_computation | async-start | bytes 8388608
  153.4 3.4 %slice-start.1 = ((s8[7077888]{0:T(1024)(128)(4,1)}), s8[2883584]{0:T(1024)(128)(4,1)S(1)}, s32[]{:S(2)}) async-start(s8[7077888]{0:T(1024)(128)(4,1)} %bitcast.130), calls=%async_computation.1 | async-start | bytes 5767168
  166.1 13.7 %collective-permute-start.29 = (bf16[48,768]{1,0:T(8,128)(2,1)S(1)}, bf16[48,768]{1,0:T(8,128)(2,1)S(1)}, u32[]{:S(2)}, u32[]{:S(2)}) collective-permute-start(bf16[48,768]{1,0:T(8,128)(2,1)S(1)} %get-tuple-element.49), channel_id=1, source_target_pairs={{0,1},{1,2},{2,3},{3,0},{4,5},{5,6},{6,7},{7,4},{8,9},{9,10},{10,1... | collective-permute-start | bytes 221192 | tf_op jit(solution)/shard_map/ppermute | solution.py:15
  167.4 12.5 %collective-permute-start.31 = (bf16[48,768]{1,0:T(8,128)(2,1)S(1)}, bf16[48,768]{1,0:T(8,128)(2,1)S(1)}, u32[]{:S(2)}, u32[]{:S(2)}) collective-permute-start(bf16[48,768]{1,0:T(8,128)(2,1)S(1)} %get-tuple-element.50), channel_id=1, source_target_pairs={{0,3},{1,0},{2,1},{3,2},{4,7},{5,4},{6,5},{7,6},{8,11},{9,8},{10,9... | collective-permute-start | bytes 221192 | tf_op jit(solution)/shard_map/ppermute | solution.py:15
  170.1 9.7 %collective-permute-start.30 = (bf16[48,768]{1,0:T(8,128)(2,1)S(1)}, bf16[48,768]{1,0:T(8,128)(2,1)S(1)}, u32[]{:S(2)}, u32[]{:S(2)}) collective-permute-start(bf16[48,768]{1,0:T(8,128)(2,1)S(1)} %get-tuple-element.51), channel_id=1, source_target_pairs={{0,2},{1,3},{2,0},{3,1},{4,6},{5,7},{6,4},{7,5},{8,10},{9,11},{10,... | collective-permute-start | bytes 221192 | tf_op jit(solution)/shard_map/ppermute | solution.py:15
  170.3 15.1 %collective-permute-start.23 = (bf16[16,768]{1,0:T(8,128)(2,1)S(1)}, bf16[16,768]{1,0:T(8,128)(2,1)S(1)}, u32[]{:S(2)}, u32[]{:S(2)}) collective-permute-start(bf16[16,768]{1,0:T(8,128)(2,1)S(1)} %get-tuple-element.42), channel_id=1, source_target_pairs={{16,0},{32,16},{48,32},{64,48},{80,64},{96,80},{112,96},{128,112},... | collective-permute-start | bytes 73736 | tf_op jit(solution)/shard_map/ppermute | solution.py:21
  173.7 7.7 %collective-permute-start.24 = (bf16[16,768]{1,0:T(8,128)(2,1)S(1)}, bf16[16,768]{1,0:T(8,128)(2,1)S(1)}, u32[]{:S(2)}, u32[]{:S(2)}) collective-permute-start(bf16[16,768]{1,0:T(8,128)(2,1)S(1)} %get-tuple-element.43), channel_id=1, source_target_pairs={{0,16},{16,32},{32,48},{48,64},{64,80},{80,96},{96,112},{112,128},... | collective-permute-start | bytes 73736 | tf_op jit(solution)/shard_map/ppermute | solution.py:20
  179.9 5.5 %copy-start.1 = (bf16[1,256,1536]{2,1,0:T(8,128)(2,1)S(1)}, bf16[1,256,1536]{2,1,0:T(8,128)(2,1)}, u32[]{:S(2)}) copy-start(bf16[1,256,1536]{2,1,0:T(8,128)(2,1)} %param.10) | copy-start | bytes 2359300
  179.9 5.5 %copy-start.4 = (f32[1536]{0:T(1024)S(1)}, f32[1536]{0:T(1024)}, u32[]{:S(2)}) copy-start(f32[1536]{0:T(1024)} %param.11) | copy-start | bytes 18436
  179.9 3.3 %collective-permute-start.32 = (bf16[48,768]{1,0:T(8,128)(2,1)S(1)}, bf16[48,768]{1,0:T(8,128)(2,1)S(1)}, u32[]{:S(2)}, u32[]{:S(2)}) collective-permute-start(bf16[48,768]{1,0:T(8,128)(2,1)S(1)} %fusion.64), channel_id=1, source_target_pairs={{0,64},{64,0},{128,192},{192,128},{1,65},{65,1},{129,193},{193,129... | collective-permute-start | bytes 221192 | tf_op jit(solution)/shard_map/ppermute | solution.py:444
  183.2 5.3 %collective-permute-start.33 = (bf16[48,768]{1,0:T(8,128)(2,1)S(1)}, bf16[48,768]{1,0:T(8,128)(2,1)S(1)}, u32[]{:S(2)}, u32[]{:S(2)}) collective-permute-start(bf16[48,768]{1,0:T(8,128)(2,1)S(1)} %add_convert_fusion.5), channel_id=1, source_target_pairs={{0,128},{64,192},{128,0},{192,64},{1,129},{65,193},{129,1},{193,65... | collective-permute-start | bytes 221192 | tf_op jit(solution)/shard_map/ppermute | solution.py:444
  188.6 7.3 %collective-permute-start.34 = (bf16[48,768]{1,0:T(8,128)(2,1)S(1)}, bf16[48,768]{1,0:T(8,128)(2,1)S(1)}, u32[]{:S(2)}, u32[]{:S(2)}) collective-permute-start(bf16[48,768]{1,0:T(8,128)(2,1)S(1)} %add_convert_fusion.4), channel_id=1, source_target_pairs={{0,32},{32,0},{1,33},{33,1},{2,34},{34,2},{3,35},{35,3},{4,36},{36... | collective-permute-start | bytes 221192 | tf_op jit(solution)/shard_map/ppermute | solution.py:15
  195.9 3.5 %collective-permute-start.35 = (f32[48,768]{1,0:T(8,128)S(1)}, f32[48,768]{1,0:T(8,128)S(1)}, u32[]{:S(2)}, u32[]{:S(2)}) collective-permute-start(f32[48,768]{1,0:T(8,128)S(1)} %convert_add_fusion.4), channel_id=1, source_target_pairs={{0,16},{16,0},{1,17},{17,1},{2,18},{18,2},{3,19},{19,3},{4,20},{20... | collective-permute-start | bytes 442376 | tf_op jit(solution)/shard_map/ppermute | solution.py:15
